TPU v7x, 32 devices: a whole 2x2x4 slice. The times are simulated.
32 devices in a mesh: dp: 32 (over z, y, x, core).
Axes of the slice: x: 2, y: 2, z: 4, core: 2. Of those that a mesh axis runs over, the one named last changes fastest.
Arguments:
- hidden_in: bfloat16 [4096, 640], P('dp'), may hold values from -6 to 6
- segment_ids: int32 [4096], P('dp'), may hold values from 0 to 3, never falling along the last dimension, each value on 1 to 2048 neighbouring positions
- cotangent: bfloat16 [4096, 640], P('dp'), may hold values from -6 to 6
- query_weight: bfloat16 [640, 1024], P(None, 'dp'), may hold values from -0.25 to 0.25
- key_weight: bfloat16 [640, 256], P(None, 'dp'), may hold values from -0.25 to 0.25
- value_weight: bfloat16 [640, 256], P(None, 'dp'), may hold values from -0.25 to 0.25
- out_weight: bfloat16 [1024, 640], P('dp'), may hold values from -0.1875 to 0.1875
- gate_weight: bfloat16 [640, 2048], P(None, 'dp'), may hold values from -0.25 to 0.25
- up_weight: bfloat16 [640, 2048], P(None, 'dp'), may hold values from -0.25 to 0.25
- down_weight: bfloat16 [2048, 640], P('dp'), may hold values from -0.125 to 0.125
- gain_attn: float32 [640], replicated, may hold values from 0.1 to 1.9
- gain_query: float32 [256], replicated, may hold values from 0.1 to 1.9
- gain_key: float32 [256], replicated, may hold values from 0.1 to 1.9
- gain_post: float32 [640], replicated, may hold values from 0.1 to 1.9
- gain_ffw: float32 [640], replicated, may hold values from 0.1 to 1.9
- gain_final: float32 [640], replicated, may hold values from 0.1 to 1.9
Outputs:
- output: bfloat16 [4096, 640], P('dp')
- input_grad: bfloat16 [4096, 640], P('dp')
- query_grad: float32 [640, 1024], P(None, 'dp')
- key_grad: float32 [640, 256], P(None, 'dp')
- value_grad: float32 [640, 256], P(None, 'dp')
- out_grad: float32 [1024, 640], P('dp')
- gate_grad: float32 [640, 2048], P(None, 'dp')
- up_grad: float32 [640, 2048], P(None, 'dp')
- down_grad: float32 [2048, 640], P('dp')
- grad_gattn: float32 [640], replicated
- grad_gquery: float32 [256], replicated
- grad_gkey: float32 [256], replicated
- grad_gpost: float32 [640], replicated
- grad_gffw: float32 [640], replicated
- grad_gfinal: float32 [640], replicated
Inputs may be any that keep to these rules, and one draw needn't show every extreme that they name: `segment_ids`: ids never fall along the tokens; every id appears; each sequence holds 1 to 2048 tokens, one exactly 2048.
All inputs are finite; a program needn't handle non-finite values.
Results may differ from a plain program's by a relative error of at most 0.017.
Values may be sent and summed in bfloat16 or wider, within the bound.
No kernel may reach another device: no remote copies, remote signals or barrier semaphores. Data moves between devices by JAX's collectives and lax.ppermute only.
A program may use at most 128 MiB of HBM per device.

v0:
```python
import jax
import jax.numpy as jnp
from jax import lax
from jax.experimental import pallas as pl
from jax.experimental.pallas import tpu as pltpu
from jax.sharding import PartitionSpec as P


H = 4
HD = 256
WINDOW = 512

EPS = 1e-06
SCALE = 0.0625
BASE = 10000.0


f32 = jnp.float32
bf16 = jnp.bfloat16


def swap(array, mask):
    peers = lax.axis_size("dp")
    return lax.ppermute(array, "dp", [(i, i ^ mask) for i in range(peers)])


def shifted(array, by):
    peers = lax.axis_size("dp")
    pairs = [(i, i + by) for i in range(peers) if 0 <= i + by < peers]
    return lax.ppermute(array, "dp", pairs)


def plan(peers):
    quad = peers // 4
    middle = []
    mask = 2
    while mask < quad:
        middle.append(mask)
        mask = mask * 2
    return middle, quad


def widen(shard, order):
    for mask in order[:-1]:
        shard = lax.optimization_barrier(jnp.stack([shard, swap(shard, mask)]))
    return shard


def finish(shard, order):
    other = swap(shard, order[-1])
    return [shard, other, swap(shard, 1), swap(other, 1)]


def quad_swaps(shard, quad):
    return [shard] + [swap(shard, k * quad) for k in (1, 2, 3)]


def plus(left, right):
    return (left.astype(f32) + right.astype(f32)).astype(bf16)


def quad_sum(parts, quad):
    got = [swap(parts[k], k * quad).astype(f32) for k in (1, 2, 3)]
    return (parts[0].astype(f32) + got[0]) + (got[1] + got[2])


def after(array, first):
    return lax.optimization_barrier((array, first))[0]


def added(*terms):
    total = terms[0].astype(f32)
    for term in terms[1:]:
        total = total + term.astype(f32)
    return total.astype(bf16)


def rms_rate(value):
    return lax.rsqrt(jnp.mean(value * value, axis=-1, keepdims=True) + EPS)


def norm_grad(value, rate, gain, incoming):
    scaled = incoming * gain
    inner = jnp.mean(scaled * value, axis=-1, keepdims=True)
    dv = rate * (scaled - value * (rate * rate * inner))
    return dv, jnp.sum(incoming * value * rate, axis=0, keepdims=True)


def turn(value, cosine, sine):
    half = value.shape[-1] // 2
    first, second = value[:, :half], value[:, half:]
    return jnp.concatenate([first * cosine - second * sine, second * cosine + first * sine], axis=-1)


def turn_back(value, cosine, sine):
    half = value.shape[-1] // 2
    first, second = value[:, :half], value[:, half:]
    return jnp.concatenate([first * cosine + second * sine, second * cosine - first * sine], axis=-1)


def xor_blocks(vector, blocks, bits):
    rows = vector.reshape(blocks, -1)
    mask = 1
    while mask < blocks:
        pairs = rows.reshape(blocks // (2 * mask), 2, mask, -1)
        rows = jnp.where((bits & mask) != 0, pairs[:, ::-1], pairs).reshape(blocks, -1)
        mask = mask * 2
    return rows.reshape(vector.shape)


def dot_t(left, right):
    return lax.dot_general(left, right, (((1,), (1,)), ((), ())), preferred_element_type=f32)


def dot_n(left, right):
    return jnp.dot(left, right, preferred_element_type=f32)


def dot_g(left, right):
    return lax.dot_general(left, right, (((0,), (0,)), ((), ())), preferred_element_type=f32)


def attn_kernel(
    window, key_seg, seg, cosine, sine, pick, q_rows, kv_slots, o_slots, gains_r,
    query_o, qrot_o, key_o, keys_o, values_o, prob_o, mixed_o, attn_o, resid_o, normed_o, kv_rows_o,
):
    g_attn, g_post, g_query, g_key = gains_r[0:1], gains_r[1:2], gains_r[4:5, :HD], gains_r[5:6, :HD]
    span = window.shape[0]
    rows = seg.shape[0]
    halo = span - rows
    wf = window[...].astype(f32)
    normed_all = (wf * rms_rate(wf) * g_attn).astype(bf16)
    normed_o[...] = normed_all
    normed = normed_all[halo:]
    k_rows = dot_n(pick[...], kv_slots[:HD]).astype(bf16)
    v_rows = dot_n(pick[...], kv_slots[HD:]).astype(bf16)
    kv_rows_o[:HD] = k_rows
    kv_rows_o[HD:] = v_rows
    key = dot_t(normed_all, k_rows)
    key_o[...] = key
    values = dot_t(normed_all, v_rows).astype(bf16)
    values_o[...] = values
    keys = turn(key * rms_rate(key) * g_key, cosine[...], sine[...]).astype(bf16)
    keys_o[...] = keys
    cos_q, sin_q = cosine[halo:], sine[halo:]
    ahead = (
        lax.broadcasted_iota(jnp.int32, (rows, span), 0)
        + halo
        - lax.broadcasted_iota(jnp.int32, (rows, span), 1)
    )
    wide = (key_seg[...] == seg[...]) & (ahead >= 0) & (ahead < WINDOW)
    attn = jnp.zeros((rows, window.shape[1]), f32)
    for h in range(H):
        cols = slice(h * HD, (h + 1) * HD)
        query = dot_t(normed, q_rows[cols, :])
        query_o[:, cols] = query
        qrot = (turn(query * rms_rate(query) * g_query, cos_q, sin_q) * SCALE).astype(bf16)
        qrot_o[:, cols] = qrot
        scores = dot_t(qrot, keys)
        weight = jnp.where(wide, jnp.exp(scores), 0.0)
        prob = weight * (1.0 / jnp.sum(weight, axis=-1, keepdims=True))
        prob_o[h] = prob
        mixed = dot_n(prob.astype(bf16), values).astype(bf16)
        mixed_o[:, cols] = mixed
        attn = attn + dot_n(mixed, o_slots[cols, :])
    attn_o[...] = attn
    resid_o[...] = wf[halo:] + attn * rms_rate(attn) * g_post


C1, C2 = 0.7978845608028654, 0.044715


def rows_of(piece, i):
    part = piece[:, i]
    return part.reshape(part.shape[0] * part.shape[1], part.shape[2])


def ff_half(pieces, grads, kept, ffw_in, d_ffw_b, d_ffwin):
    for p in (3, 1, 2, 0):
        gate, up, hidden = kept(p)
        w_gate, w_up, w_down = (rows_of(pieces[p], i) for i in range(3))
        d_hidden = dot_t(d_ffw_b, w_down)
        t = jnp.tanh(C1 * (gate + C2 * (gate * gate * gate)))
        slope = 0.5 * (1.0 + t) + 0.5 * gate * (1.0 - t * t) * (C1 * (1.0 + 3.0 * C2 * gate * gate))
        d_gate = (d_hidden * up * slope).astype(bf16)
        d_up = (d_hidden * (0.5 * gate * (1.0 + t))).astype(bf16)
        for i, (left, right) in enumerate(((d_gate, ffw_in), (d_up, ffw_in), (hidden, d_ffw_b))):
            out = grads[p]
            out[:, i] = dot_g(left, right).astype(bf16).reshape(out.shape[0], out.shape[2], out.shape[3])
        d_ffwin = d_ffwin + dot_n(d_gate, w_gate) + dot_n(d_up, w_up)
    return d_ffwin


def ff_kernel(*refs):
    resid_r, cot_r, gains_r = refs[:3]
    g_ffw, g_final = gains_r[2:3], gains_r[3:4]
    pieces = refs[3:11]
    output_o, ffw_in_o, d_ffw_o, d_ffwin_o, gains_o = refs[11:16]
    grads = refs[16:20]
    gate_o, up_o, hidden_o, gate_s, up_s, hidden_s = refs[20:]
    resid = resid_r[...]
    cot = cot_r[...].astype(f32)
    ffw_in = (resid * rms_rate(resid) * g_ffw).astype(bf16)
    ffw_in_o[...] = ffw_in
    ffw_out = jnp.zeros(resid.shape, f32)
    for p in range(8):
        gate_d, up_d, hidden_d = ((gate_s, up_s, hidden_s), (gate_o, up_o, hidden_o))[p // 4]
        gate = dot_t(ffw_in, rows_of(pieces[p], 0))
        up = dot_t(ffw_in, rows_of(pieces[p], 1))
        t = jnp.tanh(C1 * (gate + C2 * (gate * gate * gate)))
        hidden = (0.5 * gate * (1.0 + t) * up).astype(bf16)
        gate_d[p % 4] = gate
        up_d[p % 4] = up
        hidden_d[p % 4] = hidden
        ffw_out = ffw_out + dot_n(hidden, rows_of(pieces[p], 2))
    out_rate = rms_rate(ffw_out)
    output_o[...] = (resid + ffw_out * out_rate * g_final).astype(bf16)
    d_ffw, gr_final = norm_grad(ffw_out, out_rate, g_final, cot)
    d_ffw_b = d_ffw.astype(bf16)
    d_ffw_o[...] = d_ffw_b
    gains_o[...] = gr_final
    d_ffwin_o[...] = ff_half(
        pieces[:4],
        grads,
        lambda p: (gate_s[p], up_s[p], hidden_s[p]),
        ffw_in,
        d_ffw_b,
        jnp.zeros(resid.shape, f32),
    )


def ff_rest_kernel(*refs):
    resid_r, attn_r, cot_r, gains_r, ffw_in_r, d_ffw_r, d_ffwin_r, gate_r, up_r, hidden_r = refs[:10]
    g_post, g_ffw = gains_r[1:2], gains_r[2:3]
    pieces = refs[10:14]
    d_resid_o, d_attn_o, gains_o = refs[14:17]
    grads = refs[17:]
    d_ffwin = ff_half(
        pieces,
        grads,
        lambda p: (gate_r[p], up_r[p], hidden_r[p]),
        ffw_in_r[...],
        d_ffw_r[...],
        d_ffwin_r[...],
    )
    resid = resid_r[...]
    d_res, gr_ffw = norm_grad(resid, rms_rate(resid), g_ffw, d_ffwin)
    d_resid = cot_r[...].astype(f32) + d_res
    d_resid_o[...] = d_resid
    attn = attn_r[...]
    d_attn, gr_post = norm_grad(attn, rms_rate(attn), g_post, d_resid)
    d_attn_o[...] = d_attn.astype(bf16)
    gains_o[0:1] = gr_post
    gains_o[1:2] = gr_ffw


def back_kernel(
    d_attn_r, window, normed_r, cosine, sine, pick, q_rows, kv_rows, o_slots, gains_r,
    query_r, qrot_r, key_r, keys_r, values_r, prob_r, mixed_r,
    q_grad_o, kv_grad_o, o_grad_o, d_halo_o, d_own_o, gr_attn_o, gr_head_o,
):
    g_query, g_key = gains_r[4:5, :HD], gains_r[5:6, :HD]
    span, width = window.shape
    rows = d_attn_r.shape[0]
    halo = span - rows
    d_attn = d_attn_r[...]
    normed_all = normed_r[...]
    normed = normed_all[halo:]
    keys, values = keys_r[...], values_r[...]
    cos_q, sin_q = cosine[halo:], sine[halo:]
    d_keys = jnp.zeros((span, HD), f32)
    d_values = jnp.zeros((span, HD), f32)
    d_own = jnp.zeros((rows, width), f32)
    gr_query = jnp.zeros((1, HD), f32)
    for h in range(H):
        cols = slice(h * HD, (h + 1) * HD)
        mixed = mixed_r[:, cols]
        o_grad_o[cols, :] = dot_g(mixed, d_attn).astype(bf16)
        d_mixed = dot_t(d_attn, o_slots[cols, :]).astype(bf16)
        prob = prob_r[h]
        d_probs = dot_t(d_mixed, values)
        delta = jnp.sum(d_mixed.astype(f32) * mixed.astype(f32), axis=-1, keepdims=True)
        d_scores = (prob * (d_probs - delta)).astype(bf16)
        d_qrot = dot_n(d_scores, keys) * SCALE
        d_keys = d_keys + dot_g(d_scores, qrot_r[:, cols])
        d_values = d_values + dot_g(prob.astype(bf16), d_mixed)
        query = query_r[:, cols]
        d_query, gr = norm_grad(query, rms_rate(query), g_query, turn_back(d_qrot, cos_q, sin_q))
        gr_query = gr_query + gr
        d_query_b = d_query.astype(bf16)
        q_grad_o[cols, :] = dot_g(d_query_b, normed).astype(bf16)
        d_own = d_own + dot_n(d_query_b, q_rows[cols, :])
    key = key_r[...]
    d_key, gr_key = norm_grad(key, rms_rate(key), g_key, turn_back(d_keys, cosine[...], sine[...]))
    d_key_b = d_key.astype(bf16)
    d_val_b = d_values.astype(bf16)
    kv_grad_o[:HD] = dot_g(dot_n(d_key_b, pick[...]).astype(bf16), normed_all).astype(bf16)
    kv_grad_o[HD:] = dot_g(dot_n(d_val_b, pick[...]).astype(bf16), normed_all).astype(bf16)
    d_window = dot_n(d_key_b, kv_rows[:HD]) + dot_n(d_val_b, kv_rows[HD:])
    d_halo_o[...] = d_window[:halo].astype(bf16)
    d_own = d_own + d_window[halo:]
    d_own_o[...] = d_own
    wf = window[...].astype(f32)
    scaled = wf * rms_rate(wf)
    gr_attn_o[...] = jnp.sum(scaled[:halo] * d_window[:halo], axis=0, keepdims=True) + jnp.sum(
        scaled[halo:] * d_own, axis=0, keepdims=True
    )
    gr_head_o[0:1] = gr_query
    gr_head_o[1:2] = gr_key


def call(kernel, outs, args, flops, scratch=()):
    nbytes = sum(a.size * a.dtype.itemsize for a in args) + sum(o.size * o.dtype.itemsize for o in outs)
    return pl.pallas_call(
        kernel,
        out_shape=outs,
        in_specs=[pl.BlockSpec(memory_space=pltpu.VMEM)] * len(args),
        out_specs=[pl.BlockSpec(memory_space=pltpu.VMEM)] * len(outs),
        scratch_shapes=list(scratch),
        cost_estimate=pl.CostEstimate(flops=flops, bytes_accessed=nbytes, transcendentals=0),
        compiler_params=pltpu.CompilerParams(vmem_limit_bytes=56 * 1024 * 1024),
    )(*args)


def like(shape, dtype):
    return jax.ShapeDtypeStruct(shape, dtype)


def body(
    hidden_in,
    segment_ids,
    cotangent,
    query_weight,
    key_weight,
    value_weight,
    out_weight,
    gate_weight,
    up_weight,
    down_weight,
    gain_attn,
    gain_query,
    gain_key,
    gain_post,
    gain_ffw,
    gain_final,
):
    peers = lax.axis_size("dp")
    me = lax.axis_index("dp")
    middle, quad = plan(peers)
    forth, back = middle, middle[::-1]
    count = len(middle)
    rows, width = hidden_in.shape
    reach = (WINDOW + rows - 1) // rows
    halo = reach * rows
    span = halo + rows
    q_block = query_weight.shape[1]
    k_block = key_weight.shape[1]
    f_block = gate_weight.shape[1]
    f_half = f_block // 2
    heads = q_block * peers
    twos = (2,) * count
    inner = (2,) * (count - 1)

    qt, kt, vt, gt, ut = (w.T for w in (query_weight, key_weight, value_weight, gate_weight, up_weight))
    attn_shard = jnp.concatenate([qt, kt, vt, out_weight], axis=0)
    attn_quad = jnp.stack(quad_swaps(attn_shard, quad))
    qkv = q_block + 2 * k_block

    ids = jnp.zeros((8, width), bf16).at[0, :rows].set(segment_ids.astype(bf16))
    mine = jnp.concatenate([hidden_in, ids], axis=0)
    before = [shifted(mine, hop) for hop in range(reach, 0, -1)]

    ff_shard = jnp.stack([w.reshape(2, f_half, width) for w in (gt, ut, down_weight)], axis=1)
    ff_shards = quad_swaps(ff_shard, quad)
    qkv_wide = widen(attn_quad[:, :qkv], forth)
    o_wide = widen(attn_quad[:, qkv:], back)
    small = (segment_ids, gain_attn, gain_query, gain_key, gain_post, gain_ffw, gain_final, me)
    (segment_ids, gain_attn, gain_query, gain_key, gain_post, gain_ffw, gain_final, me), qkv_wide, o_wide = (
        lax.optimization_barrier((small, qkv_wide, o_wide))
    )
    qkv_pieces = finish(qkv_wide, forth)
    o_pieces = finish(o_wide, back)
    ff_shards = after(ff_shards, (qkv_wide, o_wide))
    ff_quad = jnp.stack(ff_shards, axis=2)
    ff_quads = lax.optimization_barrier([ff_quad[0], ff_quad[1]])
    wide_a = widen(ff_quads[0], forth)
    wide_b = widen(ff_quads[1], back)
    before, qkv_pieces, o_pieces = after((before, qkv_pieces, o_pieces), (wide_a, wide_b))
    ff_a = finish(wide_a, forth)
    ff_b = finish(wide_b, back)

    tail = (count + 2, count + 3)
    to_slots = (count + 1,) + tuple(range(1, count + 1)) + (0,) + tail
    to_slots_b = (count + 1,) + tuple(range(count, 0, -1)) + (0,) + tail

    def slots(pieces, order):
        whole = jnp.stack(pieces).reshape((2, 2) + pieces[0].shape)
        return whole.transpose(order)

    qkv_slots = slots(qkv_pieces, to_slots).reshape(peers, qkv, width)
    o_slots = slots(o_pieces, to_slots_b).reshape(heads, width)
    q_rows = qkv_slots[:, :q_block].reshape(heads, width)
    kv_slots = jnp.concatenate(
        [qkv_slots[:, q_block : q_block + k_block].reshape(HD, width), qkv_slots[:, q_block + k_block :].reshape(HD, width)]
    )

    per_head = peers // H
    bits = me & (per_head - 1)
    place = jnp.arange(HD, dtype=jnp.int32)
    feature = ((place // q_block) ^ bits) * q_block + place % q_block
    source = (me ^ (feature // k_block)) * k_block + feature % k_block
    pick = lax.optimization_barrier((source[:, None] == place[None, :]).astype(bf16))
    gq = xor_blocks(gain_query, per_head, bits)
    gk = xor_blocks(gain_key, per_head, bits)
    spare = jnp.zeros((width - HD,), f32)
    gains_in = jnp.concatenate(
        [gain_attn, gain_post, gain_ffw, gain_final, gq, spare, gk, spare, jnp.zeros((2 * width,), f32)]
    ).reshape(8, width)
    half = HD // 2
    freq = jnp.power(BASE, -((feature[:half] % half).astype(f32) * (2.0 / HD)))
    theta = jnp.arange(span, dtype=jnp.int32).astype(f32)[:, None] * freq[None, :]
    cosine = jnp.cos(theta)
    sine = jnp.sin(theta) * jnp.where(feature[0] >= half, -1.0, 1.0)

    window = jnp.concatenate([b[:rows] for b in before] + [hidden_in], axis=0)
    seg = segment_ids.astype(f32)
    key_seg = jnp.concatenate([b[rows, :rows].astype(f32) for b in before] + [seg])
    key_idx = me * rows - halo + jnp.arange(span, dtype=jnp.int32)
    key_seg = jnp.where(key_idx >= 0, key_seg, -1.0)[None]

    query, qrot, key, keys, values, prob, mixed, attn, resid, normed_all, kv_rows = call(
        attn_kernel,
        [
            like((rows, heads), f32),
            like((rows, heads), bf16),
            like((span, HD), f32),
            like((span, HD), bf16),
            like((span, HD), bf16),
            like((H, rows, span), f32),
            like((rows, heads), bf16),
            like((rows, width), f32),
            like((rows, width), f32),
            like((span, width), bf16),
            like((2 * HD, width), bf16),
        ],
        (window, key_seg, seg[:, None], cosine, sine, pick, q_rows, kv_slots, o_slots, gains_in),
        flops=4_000_000_000,
    )

    def flat(piece):
        return piece.reshape(-1, 3, 4 * f_half, width)

    ff_a, ff_b = ([flat(p) for p in pieces] for pieces in (ff_a, ff_b))
    unit = ff_a[0].size // (3 * width)
    grads = [like(ff_a[0].shape, bf16)] * 4
    kept = [((4, rows, unit), f32), ((4, rows, unit), f32), ((4, rows, unit), bf16)]
    output, ffw_in, d_ffw, d_ffwin, gr_final, *rest = call(
        ff_kernel,
        [
            like((rows, width), bf16),
            like((rows, width), bf16),
            like((rows, width), bf16),
            like((rows, width), f32),
            like((1, width), f32),
        ]
        + grads
        + [like(*k) for k in kept],
        (resid, cotangent, gains_in, *ff_a, *ff_b),
        flops=4_000_000_000,
        scratch=[pltpu.VMEM(*k) for k in kept],
    )
    grads_a, kept_b = rest[:4], rest[4:]
    d_resid, d_attn, gr_two, *grads_b = call(
        ff_rest_kernel,
        [like((rows, width), f32), like((rows, width), bf16), like((2, width), f32)] + grads,
        (resid, attn, cotangent, gains_in, ffw_in, d_ffw, d_ffwin, *kept_b, *ff_b),
        flops=2_000_000_000,
    )

    q_grad, kv_grad, o_grad, d_halo, d_own, gr_attn, gr_head = call(
        back_kernel,
        [
            like((heads, width), bf16),
            like((2 * HD, width), bf16),
            like((heads, width), bf16),
            like((halo, width), bf16),
            like((rows, width), f32),
            like((1, width), f32),
            like((2, HD), f32),
        ],
        (d_attn, window, normed_all, cosine, sine, pick, q_rows, kv_rows, o_slots, gains_in)
        + (query, qrot, key, keys, values, prob, mixed),
        flops=6_000_000_000,
    )

    quads = []
    for parts, order in ((grads_a, forth), (grads_b, back)):
        far = added(parts[1], swap(parts[3], 1))
        terms = [parts[0], swap(parts[2], 1), swap(far, order[-1])]
        terms = [t.reshape(inner + (3, 4, f_half, width)) for t in terms]
        for mask in order[:-1][::-1]:
            got = swap(added(*[t[1] for t in terms]), mask)
            terms = [t[0] for t in terms] + [got]
        quads.append(terms)
    ff_ready = [[added(*[t[:, k] for t in terms]) for terms in quads] for k in range(4)]
    ff_ready = [jnp.stack(r) for r in ff_ready]
    ff_sum = quad_sum(ff_ready, quad)

    gr_query = xor_blocks(gr_head[0], per_head, bits)
    gr_key = xor_blocks(gr_head[1], per_head, bits)
    gains = jnp.concatenate([gr_two[0], gr_two[1], gr_final[0], gr_attn[0], gr_query, gr_key])
    lanes = gains.shape[0]
    tall = -(-lanes // (8 * width)) * 8
    gains = jnp.pad(gains, (0, tall * width - lanes)).reshape(tall, width).astype(bf16)

    from_slots = (count + 1,) + tuple(range(1, count + 1)) + (0,) + tail
    from_slots_b = (count + 1,) + tuple(range(count, 0, -1)) + (0,) + tail
    lead = (4,) + twos + (2,)
    kv4 = kv_grad.reshape(2, peers, k_block, width)
    qkv_parts = jnp.concatenate([q_grad.reshape(peers, q_block, width), kv4[0], kv4[1]], axis=1)
    qkv_parts = qkv_parts.reshape(lead + (qkv, width)).transpose(from_slots)
    o_parts = o_grad.reshape(lead + (q_block, width)).transpose(from_slots_b)

    def ride(part, mask):
        packed = jnp.concatenate([part.reshape(-1, width), gains], axis=0)
        got = swap(packed, mask)
        return got[:-tall].reshape(part.shape), plus(gains, got[-tall:])

    o_parts = plus(o_parts[0], swap(o_parts[1], 1))
    got, gains = ride(qkv_parts[1], 1)
    qkv_parts = plus(qkv_parts[0], got)
    for j in range(count):
        packed = jnp.concatenate([qkv_parts[1].reshape(-1, width), gains], axis=0)
        got = [swap(packed, back[j]), swap(o_parts[1], forth[j])]
        if j == 0:
            got = after(got, ff_ready[1:])
        gains = plus(gains, got[0][-tall:])
        qkv_parts = plus(qkv_parts[0], got[0][:-tall].reshape(qkv_parts.shape[1:]))
        o_parts = plus(o_parts[0], got[1])
    last = [jnp.concatenate([qkv_parts[k], o_parts[k], gains], axis=0) for k in range(4)]
    last = lax.optimization_barrier(last)
    attn_sum = quad_sum(last, quad)
    gains = attn_sum[qkv + q_block :].reshape(-1)
    sums = []
    at = 0
    for size in (width, width, width, width, HD, HD):
        sums.append(gains[at : at + size])
        at = at + size
    sum_post, sum_ffw, sum_final, sum_attn, sum_query, sum_key = sums

    returned = [shifted(d_halo[(reach - hop) * rows : (reach - hop + 1) * rows], -hop) for hop in range(1, reach + 1)]
    returned = after(returned, last)
    for part in returned:
        d_own = d_own + part.astype(f32)
    xf = hidden_in.astype(f32)
    scaled = d_own * gains_in[0:1]
    rate = lax.optimization_barrier(rms_rate(xf))
    unit_rows = lax.optimization_barrier(xf * (rate * rate))
    d_in = rate * (scaled - unit_rows * jnp.mean(scaled * xf, axis=-1, keepdims=True))
    input_grad = (d_resid + d_in).astype(bf16)

    def joined(i):
        return ff_sum[:, i].reshape(f_block, width)

    return (
        output,
        input_grad,
        attn_sum[:q_block].T,
        attn_sum[q_block : q_block + k_block].T,
        attn_sum[q_block + k_block : qkv].T,
        attn_sum[qkv : qkv + q_block],
        joined(0).T,
        joined(1).T,
        joined(2),
        sum_attn,
        sum_query,
        sum_key,
        sum_post,
        sum_ffw,
        sum_final,
    )


def solution(mesh):
    rows = P("dp", None)
    columns = P(None, "dp")
    in_specs = (rows, P("dp"), rows, columns, columns, columns, rows, columns, columns, rows) + (P(),) * 6
    out_specs = (rows, rows, columns, columns, columns, rows, columns, columns, rows) + (P(),) * 6

    return jax.shard_map(body, mesh=mesh, in_specs=in_specs, out_specs=out_specs, check_vma=False)
```

profile of v0, /device:TPU:14, one launch (start us, length us, event | category | flops | bytes accessed | tf_op | source)
XLA Modules:
  0.0 254.1 jit_solution(10057539863385668235)
XLA Ops:
  2.0 2.6 %collective-permute-start.5 = (bf16[80,640]{1,0:T(8,128)(2,1)S(1)}, bf16[80,640]{1,0:T(8,128)(2,1)S(1)}, u32[]{:S(2)}, u32[]{:S(2)}) collective-permute-start(bf16[80,640]{1,0:T(8,128)(2,1)S(1)} %get-tuple-element.224), channel_id=1, source_target_pairs={{0,16},{1,17},{2,18},{3,19},{4,20},{5,21},{6,22},{7,23},{8,24},{9,... | collective-permute-start | bytes 307208 | tf_op jit(solution)/shard_map/ppermute | solution.py:24
  7.5 2.2 collective-permute-start.16
  12.0 3.1 %collective-permute-done.6 = bf16[80,640]{1,0:T(8,128)(2,1)S(1)} collective-permute-done((bf16[80,640]{1,0:T(8,128)(2,1)S(1)}, bf16[80,640]{1,0:T(8,128)(2,1)S(1)}, u32[]{:S(2)}, u32[]{:S(2)}) %collective-permute-start.6) | collective-permute-done | bytes 102432 | tf_op jit(solution)/shard_map/ppermute | solution.py:24
  16.4 4.8 %collective-permute-done.8 = bf16[4,32,640]{2,1,0:T(8,128)(2,1)S(1)} collective-permute-done((bf16[4,32,640]{2,1,0:T(8,128)(2,1)S(1)}, bf16[4,32,640]{2,1,0:T(8,128)(2,1)S(1)}, u32[]{:S(2)}, u32[]{:S(2)}) %collective-permute-start.8) | collective-permute-done | bytes 163872 | tf_op jit(solution)/shard_map/ppermute | solution.py:24
  21.2 3.9 %collective-permute-start = (bf16[136,640]{1,0:T(8,128)(2,1)S(1)}, bf16[136,640]{1,0:T(8,128)(2,1)}, u32[]{:S(2)}, u32[]{:S(2)}) collective-permute-start(bf16[136,640]{1,0:T(8,128)(2,1)S(1)} %fusion.11), channel_id=1, source_target_pairs={{0,4},{1,5},{2,6},{3,7},{4,8},{5,9},{6,10},{7,11},{8,12},{9,13},{1... | collective-permute-start | bytes 522248 | tf_op jit(solution)/shard_map/ppermute | solution.py:30
  30.0 5.3 %collective-permute-done.17 = bf16[2,3,32,640]{3,2,1,0:T(8,128)(2,1)S(1)} collective-permute-done((bf16[2,3,32,640]{3,2,1,0:T(8,128)(2,1)S(1)}, bf16[2,3,32,640]{3,2,1,0:T(8,128)(2,1)S(1)}, u32[]{:S(2)}, u32[]{:S(2)}) %collective-permute-start.17) | collective-permute-done | bytes 245792 | tf_op jit(solution)/shard_map/ppermute | solution.py:24
  40.1 6.5 %collective-permute-start.2 = (bf16[136,640]{1,0:T(8,128)(2,1)S(1)}, bf16[136,640]{1,0:T(8,128)(2,1)S(1)}, u32[]{:S(2)}, u32[]{:S(2)}) collective-permute-start(bf16[136,640]{1,0:T(8,128)(2,1)S(1)} %fusion.11), channel_id=1, source_target_pairs={{0,2},{1,3},{2,4},{3,5},{4,6},{5,7},{6,8},{7,9},{8,10},{9,11},{10,... | collective-permute-start | bytes 522248 | tf_op jit(solution)/shard_map/ppermute | solution.py:30
  46.7 7.0 %collective-permute-done.2 = bf16[136,640]{1,0:T(8,128)(2,1)S(1)} collective-permute-done((bf16[136,640]{1,0:T(8,128)(2,1)S(1)}, bf16[136,640]{1,0:T(8,128)(2,1)S(1)}, u32[]{:S(2)}, u32[]{:S(2)}) %collective-permute-start.2) | collective-permute-done | bytes 174112 | tf_op jit(solution)/shard_map/ppermute | solution.py:30
  54.2 4.4 %collective-permute-done.12 = bf16[2,4,32,640]{3,2,1,0:T(8,128)(2,1)} collective-permute-done((bf16[2,4,32,640]{3,2,1,0:T(8,128)(2,1)S(1)}, bf16[2,4,32,640]{3,2,1,0:T(8,128)(2,1)}, u32[]{:S(2)}, u32[]{:S(2)}) %collective-permute-start.12) | collective-permute-done | bytes 327712 | tf_op jit(solution)/shard_map/ppermute | solution.py:24
  60.6 2.2 collective-permute-start.3
  64.1 3.2 %collective-permute-done.3 = bf16[136,640]{1,0:T(8,128)(2,1)S(1)} collective-permute-done((bf16[136,640]{1,0:T(8,128)(2,1)S(1)}, bf16[136,640]{1,0:T(8,128)(2,1)S(1)}, u32[]{:S(2)}, u32[]{:S(2)}) %collective-permute-start.3) | collective-permute-done | bytes 174112 | tf_op jit(solution)/shard_map/ppermute | solution.py:30
  68.7 2.8 %collective-permute-start.24 = (bf16[2,3,4,32,640]{4,3,2,1,0:T(8,128)(2,1)S(1)}, bf16[2,3,4,32,640]{4,3,2,1,0:T(8,128)(2,1)S(1)}, u32[]{:S(2)}, u32[]{:S(2)}) collective-permute-start(bf16[2,3,4,32,640]{4,3,2,1,0:T(8,128)(2,1)S(1)} %pad_maximum_fusion.6), channel_id=1, source_target_pairs={{0,1},{1,0},{2,3},{3,2},{4,5},{5,4},{6,7},{7,6},{8,9},{9,8},{10,11... | collective-permute-start | bytes 2949128 | tf_op jit(solution)/shard_map/ppermute | solution.py:24
  78.2 10.6 %collective-permute-done.23 = bf16[2,3,4,32,640]{4,3,2,1,0:T(8,128)(2,1)S(1)} collective-permute-done((bf16[2,3,4,32,640]{4,3,2,1,0:T(8,128)(2,1)S(1)}, bf16[2,3,4,32,640]{4,3,2,1,0:T(8,128)(2,1)S(1)}, u32[]{:S(2)}, u32[]{:S(2)}) %collective-permute-start.23) | collective-permute-done | bytes 983072 | tf_op jit(solution)/shard_map/ppermute | solution.py:24
  88.8 3.4 %collective-permute-start.25 = (bf16[2,3,4,32,640]{4,3,2,1,0:T(8,128)(2,1)S(1)}, bf16[2,3,4,32,640]{4,3,2,1,0:T(8,128)(2,1)S(1)}, u32[]{:S(2)}, u32[]{:S(2)}) collective-permute-start(bf16[2,3,4,32,640]{4,3,2,1,0:T(8,128)(2,1)S(1)} %collective-permute-done.23), channel_id=1, source_target_pairs={{0,1},{1,0},{2,3},{3,2},{4,5},{5,4},{6,7},{7,6},{8,9},{9,8},{10,11... | collective-permute-start | bytes 2949128 | tf_op jit(solution)/shard_map/ppermute | solution.py:24
  92.2 3.2 %collective-permute-done.20 = bf16[2,3,4,32,640]{4,3,2,1,0:T(8,128)(2,1)} collective-permute-done((bf16[2,3,4,32,640]{4,3,2,1,0:T(8,128)(2,1)S(1)}, bf16[2,3,4,32,640]{4,3,2,1,0:T(8,128)(2,1)}, u32[]{:S(2)}, u32[]{:S(2)}) %collective-permute-start.20) | collective-permute-done | bytes 983072 | tf_op jit(solution)/shard_map/ppermute | solution.py:24
  99.5 8.2 %shard_map.271 = (f32[128,1024]{1,0:T(8,128)}, bf16[128,1024]{1,0:T(8,128)(2,1)}, f32[640,256]{1,0:T(8,128)}, bf16[640,256]{1,0:T(8,128)(2,1)}, bf16[640,256]{1,...) custom-call(bf16[640,640]{1,0:T(8,128)(2,1)} %copy-done.19, ...), custom_call_target="tpu_custom_call" | custom-call | flops 4000000000 | bytes 10705920 | tf_op jit(solution)/shard_map/pallas_call | solution.py:314
  109.0 11.0 %shard_map.272 = (bf16[128,640]{1,0:T(8,128)(2,1)}, bf16[128,640]{1,0:T(8,128)(2,1)}, bf16[128,640]{1,0:T(8,128)(2,1)}, f32[128,640]{1,0:T(8,128)}, f32[1,640]{1...) custom-call(f32[128,640]{1,0:T(8,128)} %get-tuple-element.130.refs_0, ...), custom_call_target="tpu_custom_call" | custom-call | flops 4000000000 | bytes 14440960 | tf_op jit(solution)/shard_map/pallas_call | solution.py:314
  120.1 7.6 %shard_map.273 = (f32[128,640]{1,0:T(8,128)}, bf16[128,640]{1,0:T(8,128)(2,1)}, f32[2,640]{1,0:T(2,128)}, bf16[2,3,128,640]{3,2,1,0:T(8,128)(2,1)}, bf16[2,3,128...) custom-call(f32[128,640]{1,0:T(8,128)} %get-tuple-element.130.refs_0_, ...), custom_call_target="tpu_custom_call" | custom-call | flops 2000000000 | bytes 11166720 | tf_op jit(solution)/shard_map/pallas_call | solution.py:314
  128.7 11.4 %shard_map.274 = (bf16[1024,640]{1,0:T(8,128)(2,1)}, bf16[512,640]{1,0:T(8,128)(2,1)}, bf16[1024,640]{1,0:T(8,128)(2,1)}, bf16[512,640]{1,0:T(8,128)(2,1)}, f32[...) custom-call(bf16[128,640]{1,0:T(8,128)(2,1)} %get-tuple-element.140.d_attn_r, bf16[640,640]{1,0:T(8,128)(2,1)} %copy-done.19, ...), custom_call_target="tpu_custom_call" | custom-call | flops 6000000000 | bytes 13820416 | tf_op jit(solution)/shard_map/pallas_call | solution.py:314
  161.1 4.4 %collective-permute-start.27 = (bf16[128,640]{1,0:T(8,128)(2,1)S(1)}, bf16[128,640]{1,0:T(8,128)(2,1)S(1)}, u32[]{:S(2)}, u32[]{:S(2)}) collective-permute-start(bf16[128,640]{1,0:T(8,128)(2,1)S(1)} %get-tuple-element.203), channel_id=1, source_target_pairs={{2,0},{3,1},{4,2},{5,3},{6,4},{7,5},{8,6},{9,7},{10,8},{11,9},{12,... | collective-permute-start | bytes 491528 | tf_op jit(solution)/shard_map/ppermute | solution.py:30
  166.7 15.7 %collective-permute-done.36 = bf16[2,3,128,640]{3,2,1,0:T(8,128)(2,1)S(1)} collective-permute-done((bf16[2,3,128,640]{3,2,1,0:T(8,128)(2,1)S(1)}, bf16[2,3,128,640]{3,2,1,0:T(8,128)(2,1)S(1)}, u32[]{:S(2)}, u32[]{:S(2)}) %collective-permute-start.36) | collective-permute-done | bytes 983072 | tf_op jit(solution)/shard_map/ppermute | solution.py:24
  184.0 4.0 %collective-permute-start.41 = (bf16[3,4,32,640]{3,2,1,0:T(8,128)(2,1)S(1)}, bf16[3,4,32,640]{3,2,1,0:T(8,128)(2,1)S(1)}, u32[]{:S(2)}, u32[]{:S(2)}) collective-permute-start(bf16[3,4,32,640]{3,2,1,0:T(8,128)(2,1)S(1)} %bitcast.359), channel_id=1, source_target_pairs={{0,4},{1,5},{2,6},{3,7},{4,0},{5,1},{6,2},{7,3},{8,12},{9,13},{10,... | collective-permute-start | bytes 1474568 | tf_op jit(solution)/shard_map/ppermute | solution.py:24
  188.1 13.3 %collective-permute-done.37 = bf16[3,4,32,640]{3,2,0,1:T(8,128)(2,1)S(1)} collective-permute-done((bf16[3,4,32,640]{3,2,0,1:T(8,128)(2,1)S(1)}, bf16[3,4,32,640]{3,2,0,1:T(8,128)(2,1)S(1)}, u32[]{:S(2)}, u32[]{:S(2)}) %collective-permute-start.37) | collective-permute-done | bytes 491552 | tf_op jit(solution)/shard_map/ppermute | solution.py:24
  203.7 4.1 %collective-permute-start.49 = (bf16[2,3,32,640]{3,2,1,0:T(8,128)(2,1)S(1)}, bf16[2,3,32,640]{3,2,1,0:T(8,128)(2,1)S(1)}, u32[]{:S(2)}, u32[]{:S(2)}) collective-permute-start(bf16[2,3,32,640]{3,2,1,0:T(8,128)(2,1)S(1)} %pad_maximum_fusion.16), channel_id=1, source_target_pairs={{0,24},{1,25},{2,26},{3,27},{4,28},{5,29},{6,30},{7,31},{8,16},{9,... | collective-permute-start | bytes 737288 | tf_op jit(solution)/shard_map/ppermute | solution.py:24
  208.0 5.9 %collective-permute-done.31 = bf16[392,640]{1,0:T(8,128)(2,1)S(1)} collective-permute-done((bf16[392,640]{1,0:T(8,128)(2,1)S(1)}, bf16[392,640]{1,0:T(8,128)(2,1)S(1)}, u32[]{:S(2)}, u32[]{:S(2)}) %collective-permute-start.31) | collective-permute-done | bytes 501792 | tf_op jit(solution)/shard_map/ppermute | solution.py:24
  216.1 3.4 %collective-permute-done.43 = bf16[4,32,640]{2,1,0:T(8,128)(2,1)S(1)} collective-permute-done((bf16[4,32,640]{2,1,0:T(8,128)(2,1)S(1)}, bf16[4,32,640]{2,1,0:T(8,128)(2,1)S(1)}, u32[]{:S(2)}, u32[]{:S(2)}) %collective-permute-start.43) | collective-permute-done | bytes 163872 | tf_op jit(solution)/shard_map/ppermute | solution.py:24
  222.2 3.0 %collective-permute-done.48 = bf16[2,3,32,640]{3,2,1,0:T(8,128)(2,1)S(1)} collective-permute-done((bf16[2,3,32,640]{3,2,1,0:T(8,128)(2,1)S(1)}, bf16[2,3,32,640]{3,2,1,0:T(8,128)(2,1)S(1)}, u32[]{:S(2)}, u32[]{:S(2)}) %collective-permute-start.48) | collective-permute-done | bytes 245792 | tf_op jit(solution)/shard_map/ppermute | solution.py:24
  225.2 2.9 %collective-permute-start.29 = (bf16[128,640]{1,0:T(8,128)(2,1)S(1)}, bf16[128,640]{1,0:T(8,128)(2,1)S(1)}, u32[]{:S(2)}, u32[]{:S(2)}) collective-permute-start(bf16[128,640]{1,0:T(8,128)(2,1)S(1)} %get-tuple-element.201), channel_id=1, source_target_pairs={{4,0},{5,1},{6,2},{7,3},{8,4},{9,5},{10,6},{11,7},{12,8},{13,9},{1... | collective-permute-start | bytes 491528 | tf_op jit(solution)/shard_map/ppermute | solution.py:30
  229.7 6.1 %collective-permute-done.42 = bf16[200,640]{1,0:T(8,128)(2,1)S(1)} collective-permute-done((bf16[200,640]{1,0:T(8,128)(2,1)S(1)}, bf16[200,640]{1,0:T(8,128)(2,1)S(1)}, u32[]{:S(2)}, u32[]{:S(2)}) %collective-permute-start.42) | collective-permute-done | bytes 256032 | tf_op jit(solution)/shard_map/ppermute | solution.py:24
  237.3 4.6 %collective-permute-start.45 = (bf16[88,640]{1,0:T(8,128)(2,1)S(1)}, bf16[88,640]{1,0:T(8,128)(2,1)S(1)}, u32[]{:S(2)}, u32[]{:S(2)}) collective-permute-start(bf16[88,640]{1,0:T(8,128)(2,1)S(1)} %get-tuple-element.171), channel_id=1, source_target_pairs={{0,16},{1,17},{2,18},{3,19},{4,20},{5,21},{6,22},{7,23},{8,24},{9,... | collective-permute-start | bytes 337928 | tf_op jit(solution)/shard_map/ppermute | solution.py:24
  243.7 5.8 %collective-permute-done.45 = bf16[88,640]{1,0:T(8,128)(2,1)S(1)} collective-permute-done((bf16[88,640]{1,0:T(8,128)(2,1)S(1)}, bf16[88,640]{1,0:T(8,128)(2,1)S(1)}, u32[]{:S(2)}, u32[]{:S(2)}) %collective-permute-start.45) | collective-permute-done | bytes 112672 | tf_op jit(solution)/shard_map/ppermute | solution.py:24
  249.5 2.1 collective-permute-done.46
  (292 shorter events, 72.9 us)
Async XLA Ops:
  6.1 22.1 %collective-permute-start.15 = (bf16[2,3,32,640]{3,2,1,0:T(8,128)(2,1)S(1)}, bf16[2,3,32,640]{3,2,1,0:T(8,128)(2,1)S(1)}, u32[]{:S(2)}, u32[]{:S(2)}) collective-permute-start(bf16[2,3,32,640]{3,2,1,0:T(8,128)(2,1)S(1)} %pad_maximum_fusion.13), channel_id=1, source_target_pairs={{0,8},{1,9},{2,10},{3,11},{4,12},{5,13},{6,14},{7,15},{8,0},{9,1},... | collective-permute-start | bytes 737288 | tf_op jit(solution)/shard_map/ppermute | solution.py:24
  7.5 22.5 %collective-permute-start.16 = (bf16[2,3,32,640]{3,2,1,0:T(8,128)(2,1)S(1)}, bf16[2,3,32,640]{3,2,1,0:T(8,128)(2,1)S(1)}, u32[]{:S(2)}, u32[]{:S(2)}) collective-permute-start(bf16[2,3,32,640]{3,2,1,0:T(8,128)(2,1)S(1)} %pad_maximum_fusion.13), channel_id=1, source_target_pairs={{0,16},{1,17},{2,18},{3,19},{4,20},{5,21},{6,22},{7,23},{8,24},{9,... | collective-permute-start | bytes 737288 | tf_op jit(solution)/shard_map/ppermute | solution.py:24
  11.3 24.0 %collective-permute-start.17 = (bf16[2,3,32,640]{3,2,1,0:T(8,128)(2,1)S(1)}, bf16[2,3,32,640]{3,2,1,0:T(8,128)(2,1)S(1)}, u32[]{:S(2)}, u32[]{:S(2)}) collective-permute-start(bf16[2,3,32,640]{3,2,1,0:T(8,128)(2,1)S(1)} %pad_maximum_fusion.13), channel_id=1, source_target_pairs={{0,24},{1,25},{2,26},{3,27},{4,28},{5,29},{6,30},{7,31},{8,16},{9,... | collective-permute-start | bytes 737288 | tf_op jit(solution)/shard_map/ppermute | solution.py:24
  21.2 18.9 %collective-permute-start = (bf16[136,640]{1,0:T(8,128)(2,1)S(1)}, bf16[136,640]{1,0:T(8,128)(2,1)}, u32[]{:S(2)}, u32[]{:S(2)}) collective-permute-start(bf16[136,640]{1,0:T(8,128)(2,1)S(1)} %fusion.11), channel_id=1, source_target_pairs={{0,4},{1,5},{2,6},{3,7},{4,8},{5,9},{6,10},{7,11},{8,12},{9,13},{1... | collective-permute-start | bytes 522248 | tf_op jit(solution)/shard_map/ppermute | solution.py:30
  25.2 21.5 %collective-permute-start.1 = (bf16[136,640]{1,0:T(8,128)(2,1)S(1)}, bf16[136,640]{1,0:T(8,128)(2,1)}, u32[]{:S(2)}, u32[]{:S(2)}) collective-permute-start(bf16[136,640]{1,0:T(8,128)(2,1)S(1)} %fusion.11), channel_id=1, source_target_pairs={{0,3},{1,4},{2,5},{3,6},{4,7},{5,8},{6,9},{7,10},{8,11},{9,12},{10... | collective-permute-start | bytes 522248 | tf_op jit(solution)/shard_map/ppermute | solution.py:30
  28.1 25.6 %collective-permute-start.9 = (bf16[2,4,48,640]{3,2,1,0:T(8,128)(2,1)S(1)}, bf16[2,4,48,640]{3,2,1,0:T(8,128)(2,1)S(1)}, u32[]{:S(2)}, u32[]{:S(2)}) collective-permute-start(bf16[2,4,48,640]{3,2,1,0:T(8,128)(2,1)S(1)} %pad_maximum_fusion.9), channel_id=1, source_target_pairs={{0,4},{1,5},{2,6},{3,7},{4,0},{5,1},{6,2},{7,3},{8,12},{9,13},{10,... | collective-permute-start | bytes 1474568 | tf_op jit(solution)/shard_map/ppermute | solution.py:24
  35.5 23.1 %collective-permute-start.19 = (bf16[3,4,32,640]{3,2,1,0:T(8,128)(2,1)S(1)}, bf16[3,4,32,640]{3,2,1,0:T(8,128)(2,1)S(1)}, u32[]{:S(2)}, u32[]{:S(2)}) collective-permute-start(bf16[3,4,32,640]{3,2,1,0:T(8,128)(2,1)S(1)} %get-tuple-element.109), channel_id=1, source_target_pairs={{0,4},{1,5},{2,6},{3,7},{4,0},{5,1},{6,2},{7,3},{8,12},{9,13},{10,... | collective-permute-start | bytes 1474568 | tf_op jit(solution)/shard_map/ppermute | solution.py:24
  35.9 24.7 %collective-permute-start.18 = (bf16[3,4,32,640]{3,2,1,0:T(8,128)(2,1)S(1)}, bf16[3,4,32,640]{3,2,1,0:T(8,128)(2,1)S(1)}, u32[]{:S(2)}, u32[]{:S(2)}) collective-permute-start(bf16[3,4,32,640]{3,2,1,0:T(8,128)(2,1)S(1)} %get-tuple-element.108), channel_id=1, source_target_pairs={{0,2},{1,3},{2,0},{3,1},{4,6},{5,7},{6,4},{7,5},{8,10},{9,11},{10,... | collective-permute-start | bytes 1474568 | tf_op jit(solution)/shard_map/ppermute | solution.py:24
  40.1 13.6 %collective-permute-start.2 = (bf16[136,640]{1,0:T(8,128)(2,1)S(1)}, bf16[136,640]{1,0:T(8,128)(2,1)S(1)}, u32[]{:S(2)}, u32[]{:S(2)}) collective-permute-start(bf16[136,640]{1,0:T(8,128)(2,1)S(1)} %fusion.11), channel_id=1, source_target_pairs={{0,2},{1,3},{2,4},{3,5},{4,6},{5,7},{6,8},{7,9},{8,10},{9,11},{10,... | collective-permute-start | bytes 522248 | tf_op jit(solution)/shard_map/ppermute | solution.py:30
  53.7 17.8 %collective-permute-start.10 = (bf16[2,4,48,640]{3,2,1,0:T(8,128)(2,1)S(1)}, bf16[2,4,48,640]{3,2,1,0:T(8,128)(2,1)}, u32[]{:S(2)}, u32[]{:S(2)}) collective-permute-start(bf16[2,4,48,640]{3,2,1,0:T(8,128)(2,1)S(1)} %pad_maximum_fusion.9), channel_id=1, source_target_pairs={{0,1},{1,0},{2,3},{3,2},{4,5},{5,4},{6,7},{7,6},{8,9},{9,8},{10,11... | collective-permute-start | bytes 1474568 | tf_op jit(solution)/shard_map/ppermute | solution.py:24
  53.7 18.0 %collective-permute-start.11 = (bf16[2,4,48,640]{3,2,1,0:T(8,128)(2,1)S(1)}, bf16[2,4,48,640]{3,2,1,0:T(8,128)(2,1)}, u32[]{:S(2)}, u32[]{:S(2)}) collective-permute-start(bf16[2,4,48,640]{3,2,1,0:T(8,128)(2,1)S(1)} %collective-permute-done.9), channel_id=1, source_target_pairs={{0,1},{1,0},{2,3},{3,2},{4,5},{5,4},{6,7},{7,6},{8,9},{9,8},{10,11... | collective-permute-start | bytes 1474568 | tf_op jit(solution)/shard_map/ppermute | solution.py:24
  58.7 12.8 %collective-permute-start.14 = (bf16[2,4,32,640]{3,2,1,0:T(8,128)(2,1)}, bf16[2,4,32,640]{3,2,1,0:T(8,128)(2,1)}, u32[]{:S(2)}, u32[]{:S(2)}) collective-permute-start(bf16[2,4,32,640]{3,2,1,0:T(8,128)(2,1)} %collective-permute-done.12), channel_id=1, source_target_pairs={{0,1},{1,0},{2,3},{3,2},{4,5},{5,4},{6,7},{7,6},{8,9},{9,8},{10,11... | collective-permute-start | bytes 983048 | tf_op jit(solution)/shard_map/ppermute | solution.py:24
  67.3 21.4 %collective-permute-start.23 = (bf16[2,3,4,32,640]{4,3,2,1,0:T(8,128)(2,1)S(1)}, bf16[2,3,4,32,640]{4,3,2,1,0:T(8,128)(2,1)S(1)}, u32[]{:S(2)}, u32[]{:S(2)}) collective-permute-start(bf16[2,3,4,32,640]{4,3,2,1,0:T(8,128)(2,1)S(1)} %pad_maximum_fusion.6), channel_id=1, source_target_pairs={{0,2},{1,3},{2,0},{3,1},{4,6},{5,7},{6,4},{7,5},{8,10},{9,11},{10,... | collective-permute-start | bytes 2949128 | tf_op jit(solution)/shard_map/ppermute | solution.py:24
  68.7 39.1 %collective-permute-start.24 = (bf16[2,3,4,32,640]{4,3,2,1,0:T(8,128)(2,1)S(1)}, bf16[2,3,4,32,640]{4,3,2,1,0:T(8,128)(2,1)S(1)}, u32[]{:S(2)}, u32[]{:S(2)}) collective-permute-start(bf16[2,3,4,32,640]{4,3,2,1,0:T(8,128)(2,1)S(1)} %pad_maximum_fusion.6), channel_id=1, source_target_pairs={{0,1},{1,0},{2,3},{3,2},{4,5},{5,4},{6,7},{7,6},{8,9},{9,8},{10,11... | collective-permute-start | bytes 2949128 | tf_op jit(solution)/shard_map/ppermute | solution.py:24
  71.5 23.8 %collective-permute-start.20 = (bf16[2,3,4,32,640]{4,3,2,1,0:T(8,128)(2,1)S(1)}, bf16[2,3,4,32,640]{4,3,2,1,0:T(8,128)(2,1)}, u32[]{:S(2)}, u32[]{:S(2)}) collective-permute-start(bf16[2,3,4,32,640]{4,3,2,1,0:T(8,128)(2,1)S(1)} %pad_maximum_fusion.5), channel_id=1, source_target_pairs={{0,4},{1,5},{2,6},{3,7},{4,0},{5,1},{6,2},{7,3},{8,12},{9,13},{10,... | collective-permute-start | bytes 2949128 | tf_op jit(solution)/shard_map/ppermute | solution.py:24
  71.5 36.3 %collective-permute-start.21 = (bf16[2,3,4,32,640]{4,3,2,1,0:T(8,128)(2,1)S(1)}, bf16[2,3,4,32,640]{4,3,2,1,0:T(8,128)(2,1)}, u32[]{:S(2)}, u32[]{:S(2)}) collective-permute-start(bf16[2,3,4,32,640]{4,3,2,1,0:T(8,128)(2,1)S(1)} %pad_maximum_fusion.5), channel_id=1, source_target_pairs={{0,1},{1,0},{2,3},{3,2},{4,5},{5,4},{6,7},{7,6},{8,9},{9,8},{10,11... | collective-permute-start | bytes 2949128 | tf_op jit(solution)/shard_map/ppermute | solution.py:24
  88.8 19.0 %collective-permute-start.25 = (bf16[2,3,4,32,640]{4,3,2,1,0:T(8,128)(2,1)S(1)}, bf16[2,3,4,32,640]{4,3,2,1,0:T(8,128)(2,1)S(1)}, u32[]{:S(2)}, u32[]{:S(2)}) collective-permute-start(bf16[2,3,4,32,640]{4,3,2,1,0:T(8,128)(2,1)S(1)} %collective-permute-done.23), channel_id=1, source_target_pairs={{0,1},{1,0},{2,3},{3,2},{4,5},{5,4},{6,7},{7,6},{8,9},{9,8},{10,11... | collective-permute-start | bytes 2949128 | tf_op jit(solution)/shard_map/ppermute | solution.py:24
  127.7 25.5 %collective-permute-start.39 = (bf16[2,3,128,640]{3,2,1,0:T(8,128)(2,1)}, bf16[2,3,128,640]{3,2,1,0:T(8,128)(2,1)}, u32[]{:S(2)}, u32[]{:S(2)}) collective-permute-start(bf16[2,3,128,640]{3,2,1,0:T(8,128)(2,1)} %get-tuple-element.166), channel_id=1, source_target_pairs={{0,1},{1,0},{2,3},{3,2},{4,5},{5,4},{6,7},{7,6},{8,9},{9,8},{10,11... | collective-permute-start | bytes 2949128 | tf_op jit(solution)/shard_map/ppermute | solution.py:24
  128.2 29.8 %collective-permute-start.38 = (bf16[2,3,128,640]{3,2,1,0:T(8,128)(2,1)}, bf16[2,3,128,640]{3,2,1,0:T(8,128)(2,1)}, u32[]{:S(2)}, u32[]{:S(2)}) collective-permute-start(bf16[2,3,128,640]{3,2,1,0:T(8,128)(2,1)} %get-tuple-element.164), channel_id=1, source_target_pairs={{0,1},{1,0},{2,3},{3,2},{4,5},{5,4},{6,7},{7,6},{8,9},{9,8},{10,11... | collective-permute-start | bytes 2949128 | tf_op jit(solution)/shard_map/ppermute | solution.py:24
  128.5 22.7 %collective-permute-start.35 = (bf16[2,3,128,640]{3,2,1,0:T(8,128)(2,1)}, bf16[2,3,128,640]{3,2,1,0:T(8,128)(2,1)}, u32[]{:S(2)}, u32[]{:S(2)}) collective-permute-start(bf16[2,3,128,640]{3,2,1,0:T(8,128)(2,1)} %get-tuple-element.162), channel_id=1, source_target_pairs={{0,1},{1,0},{2,3},{3,2},{4,5},{5,4},{6,7},{7,6},{8,9},{9,8},{10,11... | collective-permute-start | bytes 2949128 | tf_op jit(solution)/shard_map/ppermute | solution.py:24
  151.2 14.2 %collective-permute-start.30 = (bf16[776,640]{1,0:T(8,128)(2,1)S(1)}, bf16[776,640]{1,0:T(8,128)(2,1)S(1)}, u32[]{:S(2)}, u32[]{:S(2)}) collective-permute-start(bf16[776,640]{1,0:T(8,128)(2,1)S(1)} %pad_maximum_fusion.3), channel_id=1, source_target_pairs={{0,1},{1,0},{2,3},{3,2},{4,5},{5,4},{6,7},{7,6},{8,9},{9,8},{10,11... | collective-permute-start | bytes 2979848 | tf_op jit(solution)/shard_map/ppermute | solution.py:24
  153.1 29.2 %collective-permute-start.36 = (bf16[2,3,128,640]{3,2,1,0:T(8,128)(2,1)S(1)}, bf16[2,3,128,640]{3,2,1,0:T(8,128)(2,1)S(1)}, u32[]{:S(2)}, u32[]{:S(2)}) collective-permute-start(bf16[2,3,128,640]{3,2,1,0:T(8,128)(2,1)S(1)} %add_convert_fusion.1), channel_id=1, source_target_pairs={{0,4},{1,5},{2,6},{3,7},{4,0},{5,1},{6,2},{7,3},{8,12},{9,13},{10,... | collective-permute-start | bytes 2949128 | tf_op jit(solution)/shard_map/ppermute | solution.py:24
  155.0 27.7 %collective-permute-start.40 = (bf16[2,3,128,640]{3,2,1,0:T(8,128)(2,1)S(1)}, bf16[2,3,128,640]{3,2,1,0:T(8,128)(2,1)S(1)}, u32[]{:S(2)}, u32[]{:S(2)}) collective-permute-start(bf16[2,3,128,640]{3,2,1,0:T(8,128)(2,1)S(1)} %add_convert_fusion), channel_id=1, source_target_pairs={{0,2},{1,3},{2,0},{3,1},{4,6},{5,7},{6,4},{7,5},{8,10},{9,11},{10,... | collective-permute-start | bytes 2949128 | tf_op jit(solution)/shard_map/ppermute | solution.py:24
  158.1 79.2 %collective-permute-start.26 = (bf16[128,640]{1,0:T(8,128)(2,1)S(1)}, bf16[128,640]{1,0:T(8,128)(2,1)S(1)}, u32[]{:S(2)}, u32[]{:S(2)}) collective-permute-start(bf16[128,640]{1,0:T(8,128)(2,1)S(1)} %get-tuple-element.204), channel_id=1, source_target_pairs={{1,0},{2,1},{3,2},{4,3},{5,4},{6,5},{7,6},{8,7},{9,8},{10,9},{11,1... | collective-permute-start | bytes 491528 | tf_op jit(solution)/shard_map/ppermute | solution.py:30
  161.1 80.8 %collective-permute-start.27 = (bf16[128,640]{1,0:T(8,128)(2,1)S(1)}, bf16[128,640]{1,0:T(8,128)(2,1)S(1)}, u32[]{:S(2)}, u32[]{:S(2)}) collective-permute-start(bf16[128,640]{1,0:T(8,128)(2,1)S(1)} %get-tuple-element.203), channel_id=1, source_target_pairs={{2,0},{3,1},{4,2},{5,3},{6,4},{7,5},{8,6},{9,7},{10,8},{11,9},{12,... | collective-permute-start | bytes 491528 | tf_op jit(solution)/shard_map/ppermute | solution.py:30
  165.5 42.4 %collective-permute-start.33 = (bf16[2,4,32,640]{3,2,1,0:T(8,128)(2,1)S(1)}, bf16[2,4,32,640]{3,2,1,0:T(8,128)(2,1)S(1)}, u32[]{:S(2)}, u32[]{:S(2)}) collective-permute-start(bf16[2,4,32,640]{3,2,1,0:T(8,128)(2,1)S(1)} %slice_bitcast_fusion.7), channel_id=1, source_target_pairs={{0,2},{1,3},{2,0},{3,1},{4,6},{5,7},{6,4},{7,5},{8,10},{9,11},{10,... | collective-permute-start | bytes 983048 | tf_op jit(solution)/shard_map/ppermute | solution.py:24
  182.6 18.9 %collective-permute-start.37 = (bf16[3,4,32,640]{3,2,0,1:T(8,128)(2,1)S(1)}, bf16[3,4,32,640]{3,2,0,1:T(8,128)(2,1)S(1)}, u32[]{:S(2)}, u32[]{:S(2)}) collective-permute-start(bf16[3,4,32,640]{3,2,0,1:T(8,128)(2,1)S(1)} %copy.47), channel_id=1, source_target_pairs={{0,2},{1,3},{2,0},{3,1},{4,6},{5,7},{6,4},{7,5},{8,10},{9,11},{10,... | collective-permute-start | bytes 1474568 | tf_op jit(solution)/shard_map/ppermute | solution.py:24
  184.0 19.5 %collective-permute-start.41 = (bf16[3,4,32,640]{3,2,1,0:T(8,128)(2,1)S(1)}, bf16[3,4,32,640]{3,2,1,0:T(8,128)(2,1)S(1)}, u32[]{:S(2)}, u32[]{:S(2)}) collective-permute-start(bf16[3,4,32,640]{3,2,1,0:T(8,128)(2,1)S(1)} %bitcast.359), channel_id=1, source_target_pairs={{0,4},{1,5},{2,6},{3,7},{4,0},{5,1},{6,2},{7,3},{8,12},{9,13},{10,... | collective-permute-start | bytes 1474568 | tf_op jit(solution)/shard_map/ppermute | solution.py:24
  203.7 16.6 %collective-permute-start.49 = (bf16[2,3,32,640]{3,2,1,0:T(8,128)(2,1)S(1)}, bf16[2,3,32,640]{3,2,1,0:T(8,128)(2,1)S(1)}, u32[]{:S(2)}, u32[]{:S(2)}) collective-permute-start(bf16[2,3,32,640]{3,2,1,0:T(8,128)(2,1)S(1)} %pad_maximum_fusion.16), channel_id=1, source_target_pairs={{0,24},{1,25},{2,26},{3,27},{4,28},{5,29},{6,30},{7,31},{8,16},{9,... | collective-permute-start | bytes 737288 | tf_op jit(solution)/shard_map/ppermute | solution.py:24
  207.9 17.3 %collective-permute-start.48 = (bf16[2,3,32,640]{3,2,1,0:T(8,128)(2,1)S(1)}, bf16[2,3,32,640]{3,2,1,0:T(8,128)(2,1)S(1)}, u32[]{:S(2)}, u32[]{:S(2)}) collective-permute-start(bf16[2,3,32,640]{3,2,1,0:T(8,128)(2,1)S(1)} %pad_maximum_fusion.15), channel_id=1, source_target_pairs={{0,16},{1,17},{2,18},{3,19},{4,20},{5,21},{6,22},{7,23},{8,24},{9,... | collective-permute-start | bytes 737288 | tf_op jit(solution)/shard_map/ppermute | solution.py:24
  220.3 22.1 %collective-permute-start.28 = (bf16[128,640]{1,0:T(8,128)(2,1)S(1)}, bf16[128,640]{1,0:T(8,128)(2,1)S(1)}, u32[]{:S(2)}, u32[]{:S(2)}) collective-permute-start(bf16[128,640]{1,0:T(8,128)(2,1)S(1)} %get-tuple-element.202), channel_id=1, source_target_pairs={{3,0},{4,1},{5,2},{6,3},{7,4},{8,5},{9,6},{10,7},{11,8},{12,9},{13... | collective-permute-start | bytes 491528 | tf_op jit(solution)/shard_map/ppermute | solution.py:30
  225.2 17.2 %collective-permute-start.29 = (bf16[128,640]{1,0:T(8,128)(2,1)S(1)}, bf16[128,640]{1,0:T(8,128)(2,1)S(1)}, u32[]{:S(2)}, u32[]{:S(2)}) collective-permute-start(bf16[128,640]{1,0:T(8,128)(2,1)S(1)} %get-tuple-element.201), channel_id=1, source_target_pairs={{4,0},{5,1},{6,2},{7,3},{8,4},{9,5},{10,6},{11,7},{12,8},{13,9},{1... | collective-permute-start | bytes 491528 | tf_op jit(solution)/shard_map/ppermute | solution.py:30
  (55 other events, 409.3 us)
where the time goes:
time: 257 us; the launch traced here: 254 us
  waiting for transfers between devices  99.5 us (39%)
  starting transfers between devices  68 us (26%)
  Pallas kernels  38.3 us (15%)
  other arithmetic  23.8 us (9%)
  local copies, waits for them, and re-layouts  22.1 us (9%)
    ppermute x42, waiting for transfers between devices, swap(): return lax.ppermute(array, 'dp', [(i, i ^ mask) for i in range(peers)])  89.4 us
    ppermute x42, starting transfers between devices, swap(): return lax.ppermute(array, 'dp', [(i, i ^ mask) for i in range(peers)])  42.3 us
    pallas_call x4, Pallas kernels, call(): pl.pallas_call(kernel, out_shape=outs, in_specs=[pl.BlockSpec(memory_spac...  38.3 us
    ppermute x8, starting transfers between devices, shifted(): return lax.ppermute(array, 'dp', pairs)  25.7 us
    ppermute x8, waiting for transfers between devices, shifted(): return lax.ppermute(array, 'dp', pairs)  10.2 us
    unnamed x87, local copies, waits for them, and re-layouts  5.34 us
  transfers between devices with their start and end apart: 50, of which 19 were waited for; matrix products, arithmetic and copies ran while one was open for 16% of the time, Pallas kernels for 8%

commit v1 on v0

--- a/solution.py
+++ b/solution.py
@@ -120,13 +120,18 @@
     return lax.dot_general(left, right, (((0,), (0,)), ((), ())), preferred_element_type=f32)
 
 
-def attn_kernel(
-    window, key_seg, seg, cosine, sine, pick, q_rows, kv_slots, o_slots, gains_r,
-    query_o, qrot_o, key_o, keys_o, values_o, prob_o, mixed_o, attn_o, resid_o, normed_o, kv_rows_o,
-):
+def attn_kernel(*refs):
+    (
+        mine, seg, cosine, sine, pick, q_rows, kv_slots, o_slots, gains_r,
+        query_o, qrot_o, key_o, keys_o, values_o, prob_o, mixed_o, attn_o, resid_o, normed_o, kv_rows_o, window,
+    ) = refs[-21:]
+    parts = refs[:-21] + (mine,)
     g_attn, g_post, g_query, g_key = gains_r[0:1], gains_r[1:2], gains_r[4:5, :HD], gains_r[5:6, :HD]
     span = window.shape[0]
     rows = seg.shape[0]
+    for i, part in enumerate(parts):
+        window[i * rows : (i + 1) * rows, :] = part[:rows, :]
+    key_seg = jnp.concatenate([part[rows : rows + 8, :rows].astype(f32)[0:1] for part in parts], axis=1)
     halo = span - rows
     wf = window[...].astype(f32)
     normed_all = (wf * rms_rate(wf) * g_attn).astype(bf16)
@@ -148,7 +153,7 @@
         + halo
         - lax.broadcasted_iota(jnp.int32, (rows, span), 1)
     )
-    wide = (key_seg[...] == seg[...]) & (ahead >= 0) & (ahead < WINDOW)
+    wide = (key_seg == seg[...]) & (ahead >= 0) & (ahead < WINDOW)
     attn = jnp.zeros((rows, window.shape[1]), f32)
     for h in range(H):
         cols = slice(h * HD, (h + 1) * HD)
@@ -366,9 +371,10 @@
     attn_quad = jnp.stack(quad_swaps(attn_shard, quad))
     qkv = q_block + 2 * k_block
 
-    ids = jnp.zeros((8, width), bf16).at[0, :rows].set(segment_ids.astype(bf16))
+    ids = jnp.zeros((8, width), bf16).at[0, :rows].set((segment_ids + 1).astype(bf16))
     mine = jnp.concatenate([hidden_in, ids], axis=0)
-    before = [shifted(mine, hop) for hop in range(reach, 0, -1)]
+    even = (me & 1) == 0
+    hops = [mine] + [shifted(mine, hop) for hop in range(2, reach + 1, 2)]
 
     ff_shard = jnp.stack([w.reshape(2, f_half, width) for w in (gt, ut, down_weight)], axis=1)
     ff_shards = quad_swaps(ff_shard, quad)
@@ -385,7 +391,11 @@
     ff_quads = lax.optimization_barrier([ff_quad[0], ff_quad[1]])
     wide_a = widen(ff_quads[0], forth)
     wide_b = widen(ff_quads[1], back)
-    before, qkv_pieces, o_pieces = after((before, qkv_pieces, o_pieces), (wide_a, wide_b))
+    hops, qkv_pieces, o_pieces = after((hops, qkv_pieces, o_pieces), (wide_a, wide_b))
+    theirs = swap(jnp.stack(hops), 1)
+    before = []
+    for k in range(reach // 2, 0, -1):
+        before += [hops[k], jnp.where(even, theirs[k], theirs[k - 1])]
     ff_a = finish(wide_a, forth)
     ff_b = finish(wide_b, back)
 
@@ -422,13 +432,9 @@
     cosine = jnp.cos(theta)
     sine = jnp.sin(theta) * jnp.where(feature[0] >= half, -1.0, 1.0)
 
-    window = jnp.concatenate([b[:rows] for b in before] + [hidden_in], axis=0)
-    seg = segment_ids.astype(f32)
-    key_seg = jnp.concatenate([b[rows, :rows].astype(f32) for b in before] + [seg])
-    key_idx = me * rows - halo + jnp.arange(span, dtype=jnp.int32)
-    key_seg = jnp.where(key_idx >= 0, key_seg, -1.0)[None]
-
-    query, qrot, key, keys, values, prob, mixed, attn, resid, normed_all, kv_rows = call(
+    seg = (segment_ids + 1).astype(f32)
+
+    query, qrot, key, keys, values, prob, mixed, attn, resid, normed_all, kv_rows, window = call(
         attn_kernel,
         [
             like((rows, heads), f32),
@@ -442,8 +448,9 @@
             like((rows, width), f32),
             like((span, width), bf16),
             like((2 * HD, width), bf16),
+            like((span, width), bf16),
         ],
-        (window, key_seg, seg[:, None], cosine, sine, pick, q_rows, kv_slots, o_slots, gains_in),
+        (*before, mine, seg[:, None], cosine, sine, pick, q_rows, kv_slots, o_slots, gains_in),
         flops=4_000_000_000,
     )
 
@@ -548,14 +555,22 @@
         at = at + size
     sum_post, sum_ffw, sum_final, sum_attn, sum_query, sum_key = sums
 
-    returned = [shifted(d_halo[(reach - hop) * rows : (reach - hop + 1) * rows], -hop) for hop in range(1, reach + 1)]
-    returned = after(returned, last)
-    for part in returned:
+    away = [d_halo[(reach - hop) * rows : (reach - hop + 1) * rows] for hop in range(1, reach + 1)]
+    theirs = swap(jnp.stack(away[::2]), 1)
+    zero = jnp.zeros_like(theirs[0])
+    own = jnp.where(even, theirs[0], zero)
+    returned = []
+    for k in range(1, reach // 2 + 1):
+        later = theirs[k] if k < reach // 2 else zero
+        packed = plus(away[2 * k - 1], jnp.where(even, later, theirs[k - 1]))
+        returned.append(shifted(packed, -2 * k))
+    own, returned = after((own, returned), last)
+    for part in [own] + returned:
         d_own = d_own + part.astype(f32)
     xf = hidden_in.astype(f32)
     scaled = d_own * gains_in[0:1]
     rate = lax.optimization_barrier(rms_rate(xf))
-    unit_rows = lax.optimization_barrier(xf * (rate * rate))
+    unit_rows = xf * (rate * rate)
     d_in = rate * (scaled - unit_rows * jnp.mean(scaled * xf, axis=-1, keepdims=True))
     input_grad = (d_resid + d_in).astype(bf16)
 

time: 257 us -> 234 us (0.911)
  starting transfers between devices: 68 us -> 42.8 us
    ppermute x42 -> x44, starting transfers between devices: 42.3 us -> 27.1 us  [swap(): return lax.ppermute(array, 'dp', [(i, i ^ mask) for i in range(peers)])]
    ppermute x8 -> x4, waiting for transfers between devices: 10.2 us -> 0.01 us  [shifted(): return lax.ppermute(array, 'dp', pairs)]
    ppermute x42 -> x44, waiting for transfers between devices: 89.4 us -> 99.4 us  [swap(): return lax.ppermute(array, 'dp', [(i, i ^ mask) for i in range(peers)])]
    ppermute x8 -> x4, starting transfers between devices: 25.7 us -> 15.8 us  [shifted(): return lax.ppermute(array, 'dp', pairs)]
    slice x7 -> x6, local copies, waits for them, and re-layouts: 1.25 us -> 4.99 us  [body(): terms = [t[0] for t in terms] + [got]]
    unnamed x87 -> x91, local copies, waits for them, and re-layouts: 5.34 us -> 3.95 us
  transfers between devices with their start and end apart: 50 -> 48, of which waited for: 19 -> 19; matrix products, arithmetic and copies ran while one was open for 16% -> 18% of each run, Pallas kernels for 8% -> 9%
where the time goes in v1:
time: 234 us; the launch traced here: 231 us
  waiting for transfers between devices  99.4 us (42%)
  starting transfers between devices  42.8 us (18%)
  Pallas kernels  39.2 us (17%)
  other arithmetic  24.6 us (11%)
  local copies, waits for them, and re-layouts  22.2 us (9%)
  between operations  2.46 us (1%)
    ppermute x44, waiting for transfers between devices, swap(): return lax.ppermute(array, 'dp', [(i, i ^ mask) for i in range(peers)])  99.4 us
    pallas_call x4, Pallas kernels, call(): pl.pallas_call(kernel, out_shape=outs, in_specs=[pl.BlockSpec(memory_spac...  39.2 us
    ppermute x44, starting transfers between devices, swap(): return lax.ppermute(array, 'dp', [(i, i ^ mask) for i in range(peers)])  27.1 us
    ppermute x4, starting transfers between devices, shifted(): return lax.ppermute(array, 'dp', pairs)  15.8 us
    convert_element_type x4, other arithmetic, added(): return total.astype(bf16)  5.37 us
    slice x6, local copies, waits for them, and re-layouts, body(): terms = [t[0] for t in terms] + [got]  4.99 us
  transfers between devices with their start and end apart: 48, of which 19 were waited for; matrix products, arithmetic and copies ran while one was open for 18% of the time, Pallas kernels for 9%

profile of v1, /device:TPU:14, one launch (start us, length us, event | category | flops | bytes accessed | tf_op | source)
XLA Modules:
  0.0 230.8 jit_solution(7825596559884042417)
XLA Ops:
  2.0 2.6 %collective-permute-start.3 = (bf16[80,640]{1,0:T(8,128)(2,1)S(1)}, bf16[80,640]{1,0:T(8,128)(2,1)S(1)}, u32[]{:S(2)}, u32[]{:S(2)}) collective-permute-start(bf16[80,640]{1,0:T(8,128)(2,1)S(1)} %get-tuple-element.223), channel_id=1, source_target_pairs={{0,16},{1,17},{2,18},{3,19},{4,20},{5,21},{6,22},{7,23},{8,24},{9,... | collective-permute-start | bytes 307208 | tf_op jit(solution)/shard_map/ppermute | solution.py:24
  7.5 2.2 collective-permute-start.14
  12.0 3.1 %collective-permute-done.4 = bf16[80,640]{1,0:T(8,128)(2,1)S(1)} collective-permute-done((bf16[80,640]{1,0:T(8,128)(2,1)S(1)}, bf16[80,640]{1,0:T(8,128)(2,1)S(1)}, u32[]{:S(2)}, u32[]{:S(2)}) %collective-permute-start.4) | collective-permute-done | bytes 102432 | tf_op jit(solution)/shard_map/ppermute | solution.py:24
  16.4 4.8 %collective-permute-done.6 = bf16[4,32,640]{2,1,0:T(8,128)(2,1)S(1)} collective-permute-done((bf16[4,32,640]{2,1,0:T(8,128)(2,1)S(1)}, bf16[4,32,640]{2,1,0:T(8,128)(2,1)S(1)}, u32[]{:S(2)}, u32[]{:S(2)}) %collective-permute-start.6) | collective-permute-done | bytes 163872 | tf_op jit(solution)/shard_map/ppermute | solution.py:24
  21.2 4.8 %collective-permute-start = (bf16[136,640]{1,0:T(8,128)(2,1)S(1)}, bf16[136,640]{1,0:T(8,128)(2,1)}, u32[]{:S(2)}, u32[]{:S(2)}) collective-permute-start(bf16[136,640]{1,0:T(8,128)(2,1)S(1)} %fusion.18.refs_4_), channel_id=1, source_target_pairs={{0,2},{1,3},{2,4},{3,5},{4,6},{5,7},{6,8},{7,9},{8,10},{9,11},{10,... | collective-permute-start | bytes 522248 | tf_op jit(solution)/shard_map/ppermute | solution.py:30
  26.7 3.3 %collective-permute-done.14 = bf16[2,3,32,640]{3,2,1,0:T(8,128)(2,1)S(1)} collective-permute-done((bf16[2,3,32,640]{3,2,1,0:T(8,128)(2,1)S(1)}, bf16[2,3,32,640]{3,2,1,0:T(8,128)(2,1)S(1)}, u32[]{:S(2)}, u32[]{:S(2)}) %collective-permute-start.14) | collective-permute-done | bytes 245792 | tf_op jit(solution)/shard_map/ppermute | solution.py:24
  30.0 5.3 %collective-permute-done.15 = bf16[2,3,32,640]{3,2,1,0:T(8,128)(2,1)S(1)} collective-permute-done((bf16[2,3,32,640]{3,2,1,0:T(8,128)(2,1)S(1)}, bf16[2,3,32,640]{3,2,1,0:T(8,128)(2,1)S(1)}, u32[]{:S(2)}, u32[]{:S(2)}) %collective-permute-start.15) | collective-permute-done | bytes 245792 | tf_op jit(solution)/shard_map/ppermute | solution.py:24
  37.5 10.1 %collective-permute-done.17 = bf16[3,4,32,640]{3,2,1,0:T(8,128)(2,1)S(1)} collective-permute-done((bf16[3,4,32,640]{3,2,1,0:T(8,128)(2,1)S(1)}, bf16[3,4,32,640]{3,2,1,0:T(8,128)(2,1)S(1)}, u32[]{:S(2)}, u32[]{:S(2)}) %collective-permute-start.17) | collective-permute-done | bytes 491552 | tf_op jit(solution)/shard_map/ppermute | solution.py:24
  47.6 3.5 %collective-permute-start.1 = (bf16[136,640]{1,0:T(8,128)(2,1)S(1)}, bf16[136,640]{1,0:T(8,128)(2,1)S(1)}, u32[]{:S(2)}, u32[]{:S(2)}) collective-permute-start(bf16[136,640]{1,0:T(8,128)(2,1)S(1)} %fusion.18.refs_4_), channel_id=1, source_target_pairs={{0,4},{1,5},{2,6},{3,7},{4,8},{5,9},{6,10},{7,11},{8,12},{9,13},{1... | collective-permute-start | bytes 522248 | tf_op jit(solution)/shard_map/ppermute | solution.py:30
  52.3 2.4 %pad_maximum_fusion.5 = bf16[2,3,4,32,640]{4,3,2,1,0:T(8,128)(2,1)} fusion(bf16[1,3,4,32,640]{4,3,2,1,0:T(8,128)(2,1)} %bitcast.30, bf16[1,3,4,32,640]{4,3,2,1,0:T(8,128)(2,1)S(1)} %bitcast.347), kind=kLoop, calls=%fused_computation.14 | loop fusion | flops 491520 | bytes 1966080 | tf_op jit(solution)/shard_map/stack | solution.py:45
  54.9 3.7 %collective-permute-start.22 = (bf16[2,3,4,32,640]{4,3,2,1,0:T(8,128)(2,1)S(1)}, bf16[2,3,4,32,640]{4,3,2,1,0:T(8,128)(2,1)}, u32[]{:S(2)}, u32[]{:S(2)}) collective-permute-start(bf16[2,3,4,32,640]{4,3,2,1,0:T(8,128)(2,1)S(1)} %pad_maximum_fusion.6), channel_id=1, source_target_pairs={{0,2},{1,3},{2,0},{3,1},{4,6},{5,7},{6,4},{7,5},{8,10},{9,11},{10,... | collective-permute-start | bytes 2949128 | tf_op jit(solution)/shard_map/ppermute | solution.py:24
  62.4 2.1 fusion.6
  72.0 8.8 %collective-permute-done.22 = bf16[2,3,4,32,640]{4,3,2,1,0:T(8,128)(2,1)} collective-permute-done((bf16[2,3,4,32,640]{4,3,2,1,0:T(8,128)(2,1)S(1)}, bf16[2,3,4,32,640]{4,3,2,1,0:T(8,128)(2,1)}, u32[]{:S(2)}, u32[]{:S(2)}) %collective-permute-start.22) | collective-permute-done | bytes 983072 | tf_op jit(solution)/shard_map/ppermute | solution.py:24
  80.8 1.7 collective-permute-done.19
  84.2 8.7 %shard_map.271 = (f32[128,1024]{1,0:T(8,128)}, bf16[128,1024]{1,0:T(8,128)(2,1)}, f32[640,256]{1,0:T(8,128)}, bf16[640,256]{1,0:T(8,128)(2,1)}, bf16[640,256]{1,...) custom-call(bf16[136,640]{1,0:T(8,128)(2,1)} %copy-done.22, ...), custom_call_target="tpu_custom_call" | custom-call | flops 4000000000 | bytes 11573760 | tf_op jit(solution)/shard_map/pallas_call | solution.py:319
  94.9 11.0 %shard_map.272 = (bf16[128,640]{1,0:T(8,128)(2,1)}, bf16[128,640]{1,0:T(8,128)(2,1)}, bf16[128,640]{1,0:T(8,128)(2,1)}, f32[128,640]{1,0:T(8,128)}, f32[1,640]{1...) custom-call(f32[128,640]{1,0:T(8,128)} %get-tuple-element.128.refs_0, ...), custom_call_target="tpu_custom_call" | custom-call | flops 4000000000 | bytes 14440960 | tf_op jit(solution)/shard_map/pallas_call | solution.py:319
  105.9 7.7 %shard_map.273 = (f32[128,640]{1,0:T(8,128)}, bf16[128,640]{1,0:T(8,128)(2,1)}, f32[2,640]{1,0:T(2,128)}, bf16[2,3,128,640]{3,2,1,0:T(8,128)(2,1)}, bf16[2,3,128...) custom-call(f32[128,640]{1,0:T(8,128)} %get-tuple-element.128.refs_0_, ...), custom_call_target="tpu_custom_call" | custom-call | flops 2000000000 | bytes 11166720 | tf_op jit(solution)/shard_map/pallas_call | solution.py:319
  114.2 1.9 slice.420
  117.5 11.8 %shard_map.274 = (bf16[1024,640]{1,0:T(8,128)(2,1)}, bf16[512,640]{1,0:T(8,128)(2,1)}, bf16[1024,640]{1,0:T(8,128)(2,1)}, bf16[512,640]{1,0:T(8,128)(2,1)}, f32[...) custom-call(bf16[128,640]{1,0:T(8,128)(2,1)} %get-tuple-element.138.d_attn_r, ...), custom_call_target="tpu_custom_call" | custom-call | flops 6000000000 | bytes 13820416 | tf_op jit(solution)/shard_map/pallas_call | solution.py:319
  142.0 3.6 %collective-permute-start.26 = (bf16[128,640]{1,0:T(8,128)(2,1)S(1)}, bf16[128,640]{1,0:T(8,128)(2,1)S(1)}, u32[]{:S(2)}, u32[]{:S(2)}) collective-permute-start(bf16[128,640]{1,0:T(8,128)(2,1)S(1)} %get-tuple-element.195), channel_id=1, source_target_pairs={{2,0},{3,1},{4,2},{5,3},{6,4},{7,5},{8,6},{9,7},{10,8},{11,9},{12,... | collective-permute-start | bytes 491528 | tf_op jit(solution)/shard_map/ppermute | solution.py:30
  146.6 3.9 %collective-permute-start.27 = (bf16[128,640]{1,0:T(8,128)(2,1)S(1)}, bf16[128,640]{1,0:T(8,128)(2,1)S(1)}, u32[]{:S(2)}, u32[]{:S(2)}) collective-permute-start(bf16[128,640]{1,0:T(8,128)(2,1)S(1)} %get-tuple-element.194), channel_id=1, source_target_pairs={{4,0},{5,1},{6,2},{7,3},{8,4},{9,5},{10,6},{11,7},{12,8},{13,9},{1... | collective-permute-start | bytes 491528 | tf_op jit(solution)/shard_map/ppermute | solution.py:30
  152.1 18.5 %collective-permute-done.34 = bf16[2,3,128,640]{3,2,1,0:T(8,128)(2,1)S(1)} collective-permute-done((bf16[2,3,128,640]{3,2,1,0:T(8,128)(2,1)S(1)}, bf16[2,3,128,640]{3,2,1,0:T(8,128)(2,1)S(1)}, u32[]{:S(2)}, u32[]{:S(2)}) %collective-permute-start.34) | collective-permute-done | bytes 983072 | tf_op jit(solution)/shard_map/ppermute | solution.py:24
  173.6 12.7 %collective-permute-done.35 = bf16[3,4,32,640]{3,2,0,1:T(8,128)(2,1)S(1)} collective-permute-done((bf16[3,4,32,640]{3,2,0,1:T(8,128)(2,1)S(1)}, bf16[3,4,32,640]{3,2,0,1:T(8,128)(2,1)S(1)}, u32[]{:S(2)}, u32[]{:S(2)}) %collective-permute-start.35) | collective-permute-done | bytes 491552 | tf_op jit(solution)/shard_map/ppermute | solution.py:24
  186.3 1.7 collective-permute-start.29
  189.4 9.5 %collective-permute-done.29 = bf16[392,640]{1,0:T(8,128)(2,1)S(1)} collective-permute-done((bf16[392,640]{1,0:T(8,128)(2,1)S(1)}, bf16[392,640]{1,0:T(8,128)(2,1)S(1)}, u32[]{:S(2)}, u32[]{:S(2)}) %collective-permute-start.29) | collective-permute-done | bytes 501792 | tf_op jit(solution)/shard_map/ppermute | solution.py:24
  199.2 1.7 collective-permute-start.41
  201.1 3.5 %collective-permute-done.41 = bf16[4,32,640]{2,1,0:T(8,128)(2,1)S(1)} collective-permute-done((bf16[4,32,640]{2,1,0:T(8,128)(2,1)S(1)}, bf16[4,32,640]{2,1,0:T(8,128)(2,1)S(1)}, u32[]{:S(2)}, u32[]{:S(2)}) %collective-permute-start.41) | collective-permute-done | bytes 163872 | tf_op jit(solution)/shard_map/ppermute | solution.py:24
  205.1 2.6 %collective-permute-done.46 = bf16[2,3,32,640]{3,2,1,0:T(8,128)(2,1)S(1)} collective-permute-done((bf16[2,3,32,640]{3,2,1,0:T(8,128)(2,1)S(1)}, bf16[2,3,32,640]{3,2,1,0:T(8,128)(2,1)S(1)}, u32[]{:S(2)}, u32[]{:S(2)}) %collective-permute-start.46) | collective-permute-done | bytes 245792 | tf_op jit(solution)/shard_map/ppermute | solution.py:24
  207.7 5.4 %collective-permute-done.45 = bf16[2,3,32,640]{3,2,1,0:T(8,128)(2,1)S(1)} collective-permute-done((bf16[2,3,32,640]{3,2,1,0:T(8,128)(2,1)S(1)}, bf16[2,3,32,640]{3,2,1,0:T(8,128)(2,1)S(1)}, u32[]{:S(2)}, u32[]{:S(2)}) %collective-permute-start.45) | collective-permute-done | bytes 245792 | tf_op jit(solution)/shard_map/ppermute | solution.py:24
  214.2 2.5 %collective-permute-start.42 = (bf16[88,640]{1,0:T(8,128)(2,1)S(1)}, bf16[88,640]{1,0:T(8,128)(2,1)S(1)}, u32[]{:S(2)}, u32[]{:S(2)}) collective-permute-start(bf16[88,640]{1,0:T(8,128)(2,1)S(1)} %get-tuple-element.169), channel_id=1, source_target_pairs={{0,8},{1,9},{2,10},{3,11},{4,12},{5,13},{6,14},{7,15},{8,0},{9,1},... | collective-permute-start | bytes 337928 | tf_op jit(solution)/shard_map/ppermute | solution.py:24
  220.5 5.4 %collective-permute-done.43 = bf16[88,640]{1,0:T(8,128)(2,1)S(1)} collective-permute-done((bf16[88,640]{1,0:T(8,128)(2,1)S(1)}, bf16[88,640]{1,0:T(8,128)(2,1)S(1)}, u32[]{:S(2)}, u32[]{:S(2)}) %collective-permute-start.43) | collective-permute-done | bytes 112672 | tf_op jit(solution)/shard_map/ppermute | solution.py:24
  225.9 2.4 %collective-permute-done.44 = bf16[88,640]{1,0:T(8,128)(2,1)S(1)} collective-permute-done((bf16[88,640]{1,0:T(8,128)(2,1)S(1)}, bf16[88,640]{1,0:T(8,128)(2,1)S(1)}, u32[]{:S(2)}, u32[]{:S(2)}) %collective-permute-start.44) | collective-permute-done | bytes 112672 | tf_op jit(solution)/shard_map/ppermute | solution.py:24
  (288 shorter events, 55.5 us)
Async XLA Ops:
  6.1 20.5 %collective-permute-start.13 = (bf16[2,3,32,640]{3,2,1,0:T(8,128)(2,1)S(1)}, bf16[2,3,32,640]{3,2,1,0:T(8,128)(2,1)S(1)}, u32[]{:S(2)}, u32[]{:S(2)}) collective-permute-start(bf16[2,3,32,640]{3,2,1,0:T(8,128)(2,1)S(1)} %pad_maximum_fusion.15), channel_id=1, source_target_pairs={{0,8},{1,9},{2,10},{3,11},{4,12},{5,13},{6,14},{7,15},{8,0},{9,1},... | collective-permute-start | bytes 737288 | tf_op jit(solution)/shard_map/ppermute | solution.py:24
  7.5 22.5 %collective-permute-start.14 = (bf16[2,3,32,640]{3,2,1,0:T(8,128)(2,1)S(1)}, bf16[2,3,32,640]{3,2,1,0:T(8,128)(2,1)S(1)}, u32[]{:S(2)}, u32[]{:S(2)}) collective-permute-start(bf16[2,3,32,640]{3,2,1,0:T(8,128)(2,1)S(1)} %pad_maximum_fusion.15), channel_id=1, source_target_pairs={{0,16},{1,17},{2,18},{3,19},{4,20},{5,21},{6,22},{7,23},{8,24},{9,... | collective-permute-start | bytes 737288 | tf_op jit(solution)/shard_map/ppermute | solution.py:24
  11.3 24.0 %collective-permute-start.15 = (bf16[2,3,32,640]{3,2,1,0:T(8,128)(2,1)S(1)}, bf16[2,3,32,640]{3,2,1,0:T(8,128)(2,1)S(1)}, u32[]{:S(2)}, u32[]{:S(2)}) collective-permute-start(bf16[2,3,32,640]{3,2,1,0:T(8,128)(2,1)S(1)} %pad_maximum_fusion.15), channel_id=1, source_target_pairs={{0,24},{1,25},{2,26},{3,27},{4,28},{5,29},{6,30},{7,31},{8,16},{9,... | collective-permute-start | bytes 737288 | tf_op jit(solution)/shard_map/ppermute | solution.py:24
  15.3 10.8 %collective-permute-start.5 = (bf16[4,48,640]{2,1,0:T(8,128)(2,1)S(1)}, bf16[4,48,640]{2,1,0:T(8,128)(2,1)S(1)}, u32[]{:S(2)}, u32[]{:S(2)}) collective-permute-start(bf16[4,48,640]{2,1,0:T(8,128)(2,1)S(1)} %get-tuple-element.208), channel_id=1, source_target_pairs={{0,2},{1,3},{2,0},{3,1},{4,6},{5,7},{6,4},{7,5},{8,10},{9,11},{10,... | collective-permute-start | bytes 737288 | tf_op jit(solution)/shard_map/ppermute | solution.py:24
  21.2 33.5 %collective-permute-start = (bf16[136,640]{1,0:T(8,128)(2,1)S(1)}, bf16[136,640]{1,0:T(8,128)(2,1)}, u32[]{:S(2)}, u32[]{:S(2)}) collective-permute-start(bf16[136,640]{1,0:T(8,128)(2,1)S(1)} %fusion.18.refs_4_), channel_id=1, source_target_pairs={{0,2},{1,3},{2,4},{3,5},{4,6},{5,7},{6,8},{7,9},{8,10},{9,11},{10,... | collective-permute-start | bytes 522248 | tf_op jit(solution)/shard_map/ppermute | solution.py:30
  26.5 32.1 %collective-permute-start.7 = (bf16[2,4,48,640]{3,2,1,0:T(8,128)(2,1)S(1)}, bf16[2,4,48,640]{3,2,1,0:T(8,128)(2,1)S(1)}, u32[]{:S(2)}, u32[]{:S(2)}) collective-permute-start(bf16[2,4,48,640]{3,2,1,0:T(8,128)(2,1)S(1)} %pad_maximum_fusion.10), channel_id=1, source_target_pairs={{0,4},{1,5},{2,6},{3,7},{4,0},{5,1},{6,2},{7,3},{8,12},{9,13},{10,... | collective-permute-start | bytes 1474568 | tf_op jit(solution)/shard_map/ppermute | solution.py:24
  26.6 31.9 %collective-permute-start.10 = (bf16[2,4,32,640]{3,2,1,0:T(8,128)(2,1)S(1)}, bf16[2,4,32,640]{3,2,1,0:T(8,128)(2,1)}, u32[]{:S(2)}, u32[]{:S(2)}) collective-permute-start(bf16[2,4,32,640]{3,2,1,0:T(8,128)(2,1)S(1)} %pad_maximum_fusion.12), channel_id=1, source_target_pairs={{0,2},{1,3},{2,0},{3,1},{4,6},{5,7},{6,4},{7,5},{8,10},{9,11},{10,... | collective-permute-start | bytes 983048 | tf_op jit(solution)/shard_map/ppermute | solution.py:24
  35.5 12.0 %collective-permute-start.17 = (bf16[3,4,32,640]{3,2,1,0:T(8,128)(2,1)S(1)}, bf16[3,4,32,640]{3,2,1,0:T(8,128)(2,1)S(1)}, u32[]{:S(2)}, u32[]{:S(2)}) collective-permute-start(bf16[3,4,32,640]{3,2,1,0:T(8,128)(2,1)S(1)} %get-tuple-element.108), channel_id=1, source_target_pairs={{0,4},{1,5},{2,6},{3,7},{4,0},{5,1},{6,2},{7,3},{8,12},{9,13},{10,... | collective-permute-start | bytes 1474568 | tf_op jit(solution)/shard_map/ppermute | solution.py:24
  35.9 16.3 %collective-permute-start.16 = (bf16[3,4,32,640]{3,2,1,0:T(8,128)(2,1)S(1)}, bf16[3,4,32,640]{3,2,1,0:T(8,128)(2,1)}, u32[]{:S(2)}, u32[]{:S(2)}) collective-permute-start(bf16[3,4,32,640]{3,2,1,0:T(8,128)(2,1)S(1)} %get-tuple-element.107), channel_id=1, source_target_pairs={{0,2},{1,3},{2,0},{3,1},{4,6},{5,7},{6,4},{7,5},{8,10},{9,11},{10,... | collective-permute-start | bytes 1474568 | tf_op jit(solution)/shard_map/ppermute | solution.py:24
  54.9 26.0 %collective-permute-start.22 = (bf16[2,3,4,32,640]{4,3,2,1,0:T(8,128)(2,1)S(1)}, bf16[2,3,4,32,640]{4,3,2,1,0:T(8,128)(2,1)}, u32[]{:S(2)}, u32[]{:S(2)}) collective-permute-start(bf16[2,3,4,32,640]{4,3,2,1,0:T(8,128)(2,1)S(1)} %pad_maximum_fusion.6), channel_id=1, source_target_pairs={{0,2},{1,3},{2,0},{3,1},{4,6},{5,7},{6,4},{7,5},{8,10},{9,11},{10,... | collective-permute-start | bytes 2949128 | tf_op jit(solution)/shard_map/ppermute | solution.py:24
  58.5 24.0 %collective-permute-start.19 = (bf16[2,3,4,32,640]{4,3,2,1,0:T(8,128)(2,1)}, bf16[2,3,4,32,640]{4,3,2,1,0:T(8,128)(2,1)}, u32[]{:S(2)}, u32[]{:S(2)}) collective-permute-start(bf16[2,3,4,32,640]{4,3,2,1,0:T(8,128)(2,1)} %pad_maximum_fusion.5), channel_id=1, source_target_pairs={{0,4},{1,5},{2,6},{3,7},{4,0},{5,1},{6,2},{7,3},{8,12},{9,13},{10,... | collective-permute-start | bytes 2949128 | tf_op jit(solution)/shard_map/ppermute | solution.py:24
  64.5 28.4 %collective-permute-start.23 = (bf16[2,3,4,32,640]{4,3,2,1,0:T(8,128)(2,1)S(1)}, bf16[2,3,4,32,640]{4,3,2,1,0:T(8,128)(2,1)S(1)}, u32[]{:S(2)}, u32[]{:S(2)}) collective-permute-start(bf16[2,3,4,32,640]{4,3,2,1,0:T(8,128)(2,1)S(1)} %pad_maximum_fusion.6), channel_id=1, source_target_pairs={{0,1},{1,0},{2,3},{3,2},{4,5},{5,4},{6,7},{7,6},{8,9},{9,8},{10,11... | collective-permute-start | bytes 2949128 | tf_op jit(solution)/shard_map/ppermute | solution.py:24
  64.6 28.4 %collective-permute-start.20 = (bf16[2,3,4,32,640]{4,3,2,1,0:T(8,128)(2,1)}, bf16[2,3,4,32,640]{4,3,2,1,0:T(8,128)(2,1)S(1)}, u32[]{:S(2)}, u32[]{:S(2)}) collective-permute-start(bf16[2,3,4,32,640]{4,3,2,1,0:T(8,128)(2,1)} %pad_maximum_fusion.5), channel_id=1, source_target_pairs={{0,1},{1,0},{2,3},{3,2},{4,5},{5,4},{6,7},{7,6},{8,9},{9,8},{10,11... | collective-permute-start | bytes 2949128 | tf_op jit(solution)/shard_map/ppermute | solution.py:24
  69.0 14.5 %collective-permute-start.18 = (bf16[3,136,640]{2,1,0:T(8,128)(2,1)S(1)}, bf16[3,136,640]{2,1,0:T(8,128)(2,1)S(1)}, u32[]{:S(2)}, u32[]{:S(2)}) collective-permute-start(bf16[3,136,640]{2,1,0:T(8,128)(2,1)S(1)} %pad_maximum_fusion.8), channel_id=1, source_target_pairs={{0,1},{1,0},{2,3},{3,2},{4,5},{5,4},{6,7},{7,6},{8,9},{9,8},{10,11... | collective-permute-start | bytes 1566728 | tf_op jit(solution)/shard_map/ppermute | solution.py:24
  80.8 12.2 %collective-permute-start.24 = (bf16[2,3,4,32,640]{4,3,2,1,0:T(8,128)(2,1)}, bf16[2,3,4,32,640]{4,3,2,1,0:T(8,128)(2,1)S(1)}, u32[]{:S(2)}, u32[]{:S(2)}) collective-permute-start(bf16[2,3,4,32,640]{4,3,2,1,0:T(8,128)(2,1)} %collective-permute-done.22), channel_id=1, source_target_pairs={{0,1},{1,0},{2,3},{3,2},{4,5},{5,4},{6,7},{7,6},{8,9},{9,8},{10,11... | collective-permute-start | bytes 2949128 | tf_op jit(solution)/shard_map/ppermute | solution.py:24
  82.5 10.5 %collective-permute-start.21 = (bf16[2,3,4,32,640]{4,3,2,1,0:T(8,128)(2,1)}, bf16[2,3,4,32,640]{4,3,2,1,0:T(8,128)(2,1)S(1)}, u32[]{:S(2)}, u32[]{:S(2)}) collective-permute-start(bf16[2,3,4,32,640]{4,3,2,1,0:T(8,128)(2,1)} %collective-permute-done.19), channel_id=1, source_target_pairs={{0,1},{1,0},{2,3},{3,2},{4,5},{5,4},{6,7},{7,6},{8,9},{9,8},{10,11... | collective-permute-start | bytes 2949128 | tf_op jit(solution)/shard_map/ppermute | solution.py:24
  113.5 26.0 %collective-permute-start.37 = (bf16[2,3,128,640]{3,2,1,0:T(8,128)(2,1)}, bf16[2,3,128,640]{3,2,1,0:T(8,128)(2,1)}, u32[]{:S(2)}, u32[]{:S(2)}) collective-permute-start(bf16[2,3,128,640]{3,2,1,0:T(8,128)(2,1)} %get-tuple-element.165), channel_id=1, source_target_pairs={{0,1},{1,0},{2,3},{3,2},{4,5},{5,4},{6,7},{7,6},{8,9},{9,8},{10,11... | collective-permute-start | bytes 2949128 | tf_op jit(solution)/shard_map/ppermute | solution.py:24
  114.1 27.8 %collective-permute-start.36 = (bf16[2,3,128,640]{3,2,1,0:T(8,128)(2,1)}, bf16[2,3,128,640]{3,2,1,0:T(8,128)(2,1)}, u32[]{:S(2)}, u32[]{:S(2)}) collective-permute-start(bf16[2,3,128,640]{3,2,1,0:T(8,128)(2,1)} %get-tuple-element.163), channel_id=1, source_target_pairs={{0,1},{1,0},{2,3},{3,2},{4,5},{5,4},{6,7},{7,6},{8,9},{9,8},{10,11... | collective-permute-start | bytes 2949128 | tf_op jit(solution)/shard_map/ppermute | solution.py:24
  116.1 21.8 %collective-permute-start.33 = (bf16[2,3,128,640]{3,2,1,0:T(8,128)(2,1)}, bf16[2,3,128,640]{3,2,1,0:T(8,128)(2,1)}, u32[]{:S(2)}, u32[]{:S(2)}) collective-permute-start(bf16[2,3,128,640]{3,2,1,0:T(8,128)(2,1)} %get-tuple-element.161), channel_id=1, source_target_pairs={{0,1},{1,0},{2,3},{3,2},{4,5},{5,4},{6,7},{7,6},{8,9},{9,8},{10,11... | collective-permute-start | bytes 2949128 | tf_op jit(solution)/shard_map/ppermute | solution.py:24
  116.5 30.1 %collective-permute-start.32 = (bf16[2,3,128,640]{3,2,1,0:T(8,128)(2,1)}, bf16[2,3,128,640]{3,2,1,0:T(8,128)(2,1)}, u32[]{:S(2)}, u32[]{:S(2)}) collective-permute-start(bf16[2,3,128,640]{3,2,1,0:T(8,128)(2,1)} %get-tuple-element.159), channel_id=1, source_target_pairs={{0,1},{1,0},{2,3},{3,2},{4,5},{5,4},{6,7},{7,6},{8,9},{9,8},{10,11... | collective-permute-start | bytes 2949128 | tf_op jit(solution)/shard_map/ppermute | solution.py:24
  137.9 13.8 %collective-permute-start.28 = (bf16[776,640]{1,0:T(8,128)(2,1)S(1)}, bf16[776,640]{1,0:T(8,128)(2,1)S(1)}, u32[]{:S(2)}, u32[]{:S(2)}) collective-permute-start(bf16[776,640]{1,0:T(8,128)(2,1)S(1)} %pad_maximum_fusion.3), channel_id=1, source_target_pairs={{0,1},{1,0},{2,3},{3,2},{4,5},{5,4},{6,7},{7,6},{8,9},{9,8},{10,11... | collective-permute-start | bytes 2979848 | tf_op jit(solution)/shard_map/ppermute | solution.py:24
  139.5 31.1 %collective-permute-start.34 = (bf16[2,3,128,640]{3,2,1,0:T(8,128)(2,1)S(1)}, bf16[2,3,128,640]{3,2,1,0:T(8,128)(2,1)S(1)}, u32[]{:S(2)}, u32[]{:S(2)}) collective-permute-start(bf16[2,3,128,640]{3,2,1,0:T(8,128)(2,1)S(1)} %add_convert_fusion.1), channel_id=1, source_target_pairs={{0,4},{1,5},{2,6},{3,7},{4,0},{5,1},{6,2},{7,3},{8,12},{9,13},{10,... | collective-permute-start | bytes 2949128 | tf_op jit(solution)/shard_map/ppermute | solution.py:24
  141.3 30.7 %collective-permute-start.38 = (bf16[2,3,128,640]{3,2,1,0:T(8,128)(2,1)S(1)}, bf16[2,3,128,640]{3,2,1,0:T(8,128)(2,1)S(1)}, u32[]{:S(2)}, u32[]{:S(2)}) collective-permute-start(bf16[2,3,128,640]{3,2,1,0:T(8,128)(2,1)S(1)} %add_convert_fusion), channel_id=1, source_target_pairs={{0,2},{1,3},{2,0},{3,1},{4,6},{5,7},{6,4},{7,5},{8,10},{9,11},{10,... | collective-permute-start | bytes 2949128 | tf_op jit(solution)/shard_map/ppermute | solution.py:24
  142.0 76.3 %collective-permute-start.26 = (bf16[128,640]{1,0:T(8,128)(2,1)S(1)}, bf16[128,640]{1,0:T(8,128)(2,1)S(1)}, u32[]{:S(2)}, u32[]{:S(2)}) collective-permute-start(bf16[128,640]{1,0:T(8,128)(2,1)S(1)} %get-tuple-element.195), channel_id=1, source_target_pairs={{2,0},{3,1},{4,2},{5,3},{6,4},{7,5},{8,6},{9,7},{10,8},{11,9},{12,... | collective-permute-start | bytes 491528 | tf_op jit(solution)/shard_map/ppermute | solution.py:30
  146.6 71.6 %collective-permute-start.27 = (bf16[128,640]{1,0:T(8,128)(2,1)S(1)}, bf16[128,640]{1,0:T(8,128)(2,1)S(1)}, u32[]{:S(2)}, u32[]{:S(2)}) collective-permute-start(bf16[128,640]{1,0:T(8,128)(2,1)S(1)} %get-tuple-element.194), channel_id=1, source_target_pairs={{4,0},{5,1},{6,2},{7,3},{8,4},{9,5},{10,6},{11,7},{12,8},{13,9},{1... | collective-permute-start | bytes 491528 | tf_op jit(solution)/shard_map/ppermute | solution.py:30
  151.7 37.0 %collective-permute-start.31 = (bf16[2,4,32,640]{3,2,1,0:T(8,128)(2,1)S(1)}, bf16[2,4,32,640]{3,2,1,0:T(8,128)(2,1)S(1)}, u32[]{:S(2)}, u32[]{:S(2)}) collective-permute-start(bf16[2,4,32,640]{3,2,1,0:T(8,128)(2,1)S(1)} %slice_bitcast_fusion.7), channel_id=1, source_target_pairs={{0,2},{1,3},{2,0},{3,1},{4,6},{5,7},{6,4},{7,5},{8,10},{9,11},{10,... | collective-permute-start | bytes 983048 | tf_op jit(solution)/shard_map/ppermute | solution.py:24
  171.9 14.4 %collective-permute-start.35 = (bf16[3,4,32,640]{3,2,0,1:T(8,128)(2,1)S(1)}, bf16[3,4,32,640]{3,2,0,1:T(8,128)(2,1)S(1)}, u32[]{:S(2)}, u32[]{:S(2)}) collective-permute-start(bf16[3,4,32,640]{3,2,0,1:T(8,128)(2,1)S(1)} %copy.47), channel_id=1, source_target_pairs={{0,2},{1,3},{2,0},{3,1},{4,6},{5,7},{6,4},{7,5},{8,10},{9,11},{10,... | collective-permute-start | bytes 1474568 | tf_op jit(solution)/shard_map/ppermute | solution.py:24
  173.3 14.9 %collective-permute-start.39 = (bf16[3,4,32,640]{3,2,1,0:T(8,128)(2,1)S(1)}, bf16[3,4,32,640]{3,2,1,0:T(8,128)(2,1)S(1)}, u32[]{:S(2)}, u32[]{:S(2)}) collective-permute-start(bf16[3,4,32,640]{3,2,1,0:T(8,128)(2,1)S(1)} %bitcast.377), channel_id=1, source_target_pairs={{0,4},{1,5},{2,6},{3,7},{4,0},{5,1},{6,2},{7,3},{8,12},{9,13},{10,... | collective-permute-start | bytes 1474568 | tf_op jit(solution)/shard_map/ppermute | solution.py:24
  186.3 12.6 %collective-permute-start.29 = (bf16[392,640]{1,0:T(8,128)(2,1)S(1)}, bf16[392,640]{1,0:T(8,128)(2,1)S(1)}, u32[]{:S(2)}, u32[]{:S(2)}) collective-permute-start(bf16[392,640]{1,0:T(8,128)(2,1)S(1)} %pad_maximum_fusion.9), channel_id=1, source_target_pairs={{0,4},{1,5},{2,6},{3,7},{4,0},{5,1},{6,2},{7,3},{8,12},{9,13},{10,... | collective-permute-start | bytes 1505288 | tf_op jit(solution)/shard_map/ppermute | solution.py:24
  188.5 16.2 %collective-permute-start.47 = (bf16[2,3,32,640]{3,2,1,0:T(8,128)(2,1)S(1)}, bf16[2,3,32,640]{3,2,1,0:T(8,128)(2,1)S(1)}, u32[]{:S(2)}, u32[]{:S(2)}) collective-permute-start(bf16[2,3,32,640]{3,2,1,0:T(8,128)(2,1)S(1)} %pad_maximum_fusion.18), channel_id=1, source_target_pairs={{0,24},{1,25},{2,26},{3,27},{4,28},{5,29},{6,30},{7,31},{8,16},{9,... | collective-permute-start | bytes 737288 | tf_op jit(solution)/shard_map/ppermute | solution.py:24
  188.7 18.9 %collective-permute-start.46 = (bf16[2,3,32,640]{3,2,1,0:T(8,128)(2,1)S(1)}, bf16[2,3,32,640]{3,2,1,0:T(8,128)(2,1)S(1)}, u32[]{:S(2)}, u32[]{:S(2)}) collective-permute-start(bf16[2,3,32,640]{3,2,1,0:T(8,128)(2,1)S(1)} %pad_maximum_fusion.17), channel_id=1, source_target_pairs={{0,16},{1,17},{2,18},{3,19},{4,20},{5,21},{6,22},{7,23},{8,24},{9,... | collective-permute-start | bytes 737288 | tf_op jit(solution)/shard_map/ppermute | solution.py:24
  217.5 10.7 %collective-permute-start.44 = (bf16[88,640]{1,0:T(8,128)(2,1)S(1)}, bf16[88,640]{1,0:T(8,128)(2,1)S(1)}, u32[]{:S(2)}, u32[]{:S(2)}) collective-permute-start(bf16[88,640]{1,0:T(8,128)(2,1)S(1)} %get-tuple-element.171), channel_id=1, source_target_pairs={{0,24},{1,25},{2,26},{3,27},{4,28},{5,29},{6,30},{7,31},{8,16},{9,... | collective-permute-start | bytes 337928 | tf_op jit(solution)/shard_map/ppermute | solution.py:24
  (56 other events, 385.9 us)
